TPU v7x, 32 devices: a whole 2x2x4 slice. The times are simulated.
32 devices in a mesh: ctx: 8 (over y, x, core), dp: 4 (over z).
Axes of the slice: x: 2, y: 2, z: 4, core: 2. Of those that a mesh axis runs over, the one named last changes fastest.
Arguments:
- query_rows: bfloat16 [32768, 512], P(('dp', 'ctx')), parts along dimension 0, may hold values from -12 to 12
- key_rows: bfloat16 [32768, 512], P(('dp', 'ctx')), parts along dimension 0, may hold values from -12 to 12
- value_rows: bfloat16 [32768, 512], P(('dp', 'ctx')), parts along dimension 0, may hold values from -12 to 12
Outputs:
- attended: bfloat16 [32768, 512], P(('dp', 'ctx')), parts along dimension 0
There are 4 independent parts, one for each index of `dp`. A program takes and returns all parts, laid end to end along the dimension named above; each array names one. Nothing has to cross between parts.
All inputs are finite; a program needn't handle non-finite values.
Results may differ from a plain program's by a relative error of at most 0.0038.
Values may be sent and summed in bfloat16 or wider, within the bound.
No kernel may reach another device: no remote copies, remote signals or barrier semaphores. Data moves between devices by JAX's collectives and lax.ppermute only.
A program may use at most 128 MiB of HBM per device.

v0:
```python
import functools
import math

import jax
import jax.numpy as jnp
from jax import lax
from jax.experimental import pallas as pl
from jax.experimental.pallas import tpu as pltpu
from jax.sharding import PartitionSpec as P

HEADS = 4
LEAF = 256
LEVELS = 5
HALF = LEAF // 2
BLOCKS = 4
RIM_ROWS = 576
TABLE_ROWS = 896
L1_AT = 256
L2_AT = 640
FAR_ROWS = 192
HIDDEN = -1e30


def pooled(x):
    rows = x.shape[0]
    parts = []
    start = 0
    while start < rows:
        step = 256 if rows - start >= 256 else 128
        low = lax.broadcasted_iota(jnp.int32, (step // 2, step), 0) * 2
        col = lax.broadcasted_iota(jnp.int32, (step // 2, step), 1)
        pick = jnp.where((col == low) | (col == low + 1), 0.5, 0.0).astype(jnp.bfloat16)
        parts.append(
            jnp.dot(pick, x[start : start + step], preferred_element_type=jnp.float32).astype(
                jnp.bfloat16
            )
        )
        start += step
    return jnp.concatenate(parts, axis=0) if len(parts) > 1 else parts[0]


def pool_kernel(dev_ref, k_ref, v_ref, x1_ref, i1_ref, x2_ref, y_ref, l1_ref):
    odd = dev_ref[0] % 2 == 1
    width = k_ref.shape[1]
    for side, src in enumerate((k_ref, v_ref)):
        lanes = slice(side * width, (side + 1) * width)
        l0 = src
        l1 = pooled(src[...])
        l2 = pooled(l1)
        l3 = pooled(l2)
        l4 = pooled(l3)
        l1_ref[:, lanes] = l1
        y_ref[0:128, lanes] = l3
        y_ref[128:192, lanes] = l4
        i1_ref[L2_AT:TABLE_ROWS, lanes] = l2

        @pl.when(odd)
        def _():
            x1_ref[0:256, lanes] = l0[768:1024, :]
            x1_ref[256:384, lanes] = l1[256:384]
            x1_ref[384:512, lanes] = l2[0:128]
            x1_ref[512:576, lanes] = l2[0:64]
            i1_ref[0:256, lanes] = l0[0:256, :]
            i1_ref[L1_AT:L2_AT, lanes] = l1[0:384]
            x2_ref[0:128, lanes] = l2[0:128]
            x2_ref[128:192, lanes] = l3[64:128]

        @pl.when(jnp.logical_not(odd))
        def _():
            x1_ref[0:256, lanes] = l0[0:256, :]
            x1_ref[256:512, lanes] = l1[128:384]
            x1_ref[512:576, lanes] = l2[192:256]
            i1_ref[0:256, lanes] = l0[768:1024, :]
            i1_ref[L1_AT : L1_AT + 256, lanes] = l1[256:512]
            i1_ref[L1_AT + 256 : L2_AT, lanes] = l1[0:128]
            x2_ref[0:128, lanes] = l3
            x2_ref[128:192, lanes] = l3[64:128]


def share_kernel(dev_ref, x1_ref, x2_ref, *refs):
    y_refs, (xt_ref, i2_ref, own_ref) = refs[:-3], refs[-3:]
    odd = dev_ref[0] % 2 == 1
    xt_ref[0:256, :] = x1_ref[0:256, :]
    for slot, y_ref in enumerate(y_refs):
        i2_ref[384 + 64 * slot : 448 + 64 * slot, :] = y_ref[128:192, :]
        own_ref[128 + 64 * slot : 192 + 64 * slot, :] = y_ref[128:192, :]

    @pl.when(odd)
    def _():
        l1 = jnp.concatenate([pooled(x1_ref[0:256, :]), x1_ref[256:512, :]], axis=0)
        l2 = jnp.concatenate([pooled(l1), x1_ref[512:576, :]], axis=0)
        xt_ref[L1_AT:L2_AT, :] = l1
        xt_ref[L2_AT:TABLE_ROWS, :] = l2
        i2_ref[0:128, :] = l2[0:128]
        i2_ref[128:256, :] = pooled(l2)
        i2_ref[256:384, :] = x2_ref[0:128, :]
        own_ref[0:128, :] = x2_ref[0:128, :]

    @pl.when(jnp.logical_not(odd))
    def _():
        l1 = jnp.concatenate([x1_ref[256:384, :], pooled(x1_ref[0:256, :])], axis=0)
        l2 = jnp.concatenate([x1_ref[384:512, :], pooled(l1)], axis=0)
        xt_ref[L1_AT : L1_AT + 256, :] = l1
        xt_ref[L1_AT + 256 : L2_AT, :] = l1[0:128]
        xt_ref[L2_AT:TABLE_ROWS, :] = l2
        i2_ref[0:128, :] = x2_ref[0:128, :]
        i2_ref[128:256, :] = pooled(l2)
        i2_ref[256:384, :] = y_refs[0][0:128, :]
        own_ref[0:64, :] = pooled(x2_ref[0:128, :])
        own_ref[64:128, :] = x2_ref[128:192, :]


def attend(query, segments, scale, before):
    rows = query.shape[0]
    scores = []
    peak = None
    for k_ref, _, start, count, offset in segments:
        score = lax.dot_general(
            query,
            k_ref[start : start + count, :],
            (((1,), (1,)), ((), ())),
            preferred_element_type=jnp.float32,
        )
        scores.append(score)
        top = score[:, 0:128]
        for col in range(128, count, 128):
            top = jnp.maximum(top, score[:, col : col + 128])
        if count < 128:
            top = jnp.max(score, axis=1, keepdims=True)
        top = top * scale + offset
        if top.shape[1] < 128:
            top = jnp.broadcast_to(top, (rows, 128))
        peak = top if peak is None else jnp.maximum(peak, top)
    peak = jnp.broadcast_to(jnp.max(peak, axis=1, keepdims=True), (rows, 128))
    if before is not None:
        peak = jnp.maximum(peak, before)
    out = None
    for (_, v_ref, start, count, offset), score in zip(segments, scores):
        lifted = peak - offset
        weights = []
        for col in range(0, count, 128):
            piece = score[:, col : min(col + 128, count)]
            weights.append(jnp.exp2(piece * scale - lifted[:, : piece.shape[1]]))
        weight = jnp.concatenate(weights, axis=1) if len(weights) > 1 else weights[0]
        table = jnp.concatenate(
            [v_ref[start : start + count, :], jnp.ones((count, 128), jnp.bfloat16)], axis=1
        )
        part = jnp.dot(
            weight.astype(jnp.bfloat16), table, preferred_element_type=jnp.float32
        )
        out = part if out is None else out + part
    return peak, out[:, 0:128], out[:, 128:256]


def base_two_scale(head_size):
    return math.log2(math.e) / math.sqrt(head_size)


def local_kernel(q_ref, k_ref, v_ref, l1k_ref, l1v_ref, acc_ref, peak_ref, total_ref):
    scale = base_two_scale(q_ref.shape[1])
    own = {0: ((256, 256),), 1: (), 2: ((0, 128),), 3: ((0, 256),)}
    for block in range(BLOCKS):
        low, high = max(block - 1, 0), min(block + 2, BLOCKS)
        segments = [(k_ref, v_ref, low * LEAF, (high - low) * LEAF, 0.0)]
        for start, count in own[block]:
            segments.append((l1k_ref, l1v_ref, start, count, 1.0))
        here = slice(block * LEAF, (block + 1) * LEAF)
        peak, acc, total = attend(q_ref[here, :], segments, scale, None)
        acc_ref[here, :] = acc
        peak_ref[here, :] = peak
        total_ref[here, :] = total


def remote_kernel(flow_spans, count, dev_ref, q_ref, *refs):
    (xtk, xtv, i1k, i1v, i2k, i2v, ownk, ownv, acc_ref, peak_ref, total_ref, out_ref) = refs
    scale = base_two_scale(q_ref.shape[1])
    me = dev_ref[0]
    chip = me // 2
    chips = count // 2

    def offset(level, valid):
        return jnp.where(valid, float(level), HIDDEN).astype(jnp.float32)

    left, right = me >= 1, me < count - 1
    flows = []
    for shifts in flow_spans:
        valid = False
        for shift in shifts:
            source = chip - shift // 2
            here = (source >= 0) & (source < chips)
            if shift == -4:
                here = here & (chip % 2 == 0)
            if shift == 6:
                here = here & (chip % 2 == 1)
            valid = here | valid
        flows.append(valid)

    def run(odd, lk, lv, rk, rv):
        a_ok = (me - 2 >= 0) if odd else (me + 2 < count)
        b_ok = (me + 3 < count) if odd else (me - 2 >= 0)
        c_ok = (me - 3 >= 0) if odd else (me + 3 < count)
        coarse = [
            (i2k, i2v, 128, 128, offset(3, a_ok)),
            (i2k, i2v, 256, 128, offset(3, b_ok)),
            (ownk, ownv, 0, 128, offset(3, c_ok)),
        ]
        for slot, valid in enumerate(flows):
            coarse.append((i2k, i2v, 384 + 64 * slot, 64, offset(4, valid)))
            coarse.append((ownk, ownv, 128 + 64 * slot, 64, offset(4, valid)))
        second = (
            [(lk, lv, L2_AT, 128, offset(2, left)), (rk, rv, L2_AT, 256, offset(2, right))],
            [(lk, lv, L2_AT, 256, offset(2, left)), (i2k, i2v, 0, 128, offset(2, me + 2 < count))],
        )
        edges = (
            [(lk, lv, 0, 256, offset(0, left)), (lk, lv, L1_AT, 128, offset(1, left))],
            [(lk, lv, L1_AT, 256, offset(1, left)), (rk, rv, L1_AT, 128, offset(1, right))],
            [(rk, rv, L1_AT, 256, offset(1, right))],
            [(rk, rv, 0, 256, offset(0, right)), (rk, rv, L1_AT + 256, 128, offset(1, right))],
        )
        for block in range(BLOCKS):
            here = slice(block * LEAF, (block + 1) * LEAF)
            segments = edges[block] + second[block // 2] + coarse
            before = peak_ref[here, :]
            peak, acc, total = attend(q_ref[here, :], segments, scale, before)
            factor = jnp.exp2(before - peak)
            acc = acc_ref[here, :] * factor + acc
            total = total_ref[here, :] * factor + total
            out_ref[here, :] = (acc / total).astype(out_ref.dtype)

    @pl.when(me % 2 == 1)
    def _():
        run(True, i1k, i1v, xtk, xtv)

    @pl.when(me % 2 == 0)
    def _():
        run(False, xtk, xtv, i1k, i1v)


def flow_pairs(shifts, count):
    pairs = []
    for shift in shifts:
        for source in range(count):
            target = source + shift
            if 0 <= target < count and not (shift == 6 and target // 2 % 2 == 0):
                pairs.append((source, target))
    return pairs


def far_flows(count):
    spans = []
    for low, high in ((-4, 4), (-6, 6)):
        pairs = flow_pairs((low, high), count)
        unique = len({s for s, _ in pairs}) == len(pairs) == len({t for _, t in pairs})
        spans.extend([(low, high)] if unique else [(low,), (high,)])
    return tuple(spans)


def on_device(query_rows, key_rows, value_rows):
    token_rows, width = query_rows.shape
    head_size = width // HEADS
    count = lax.axis_size("ctx")
    me = lax.axis_index("ctx").astype(jnp.int32).reshape(1)
    dtype = key_rows.dtype

    def shape(rows, columns=2 * width, kind=dtype):
        return jax.ShapeDtypeStruct((rows, columns), kind)

    smem = pl.BlockSpec(memory_space=pltpu.SMEM)
    vmem = pl.BlockSpec(memory_space=pltpu.VMEM)
    params = pltpu.CompilerParams(vmem_limit_bytes=56 << 20)

    x1s, i1s, x2s, ys, l1 = pl.pallas_call(
        pool_kernel,
        name="pool",
        out_shape=[
            shape(RIM_ROWS), shape(TABLE_ROWS), shape(FAR_ROWS), shape(192), shape(token_rows // 2)
        ],
        in_specs=[smem, vmem, vmem],
        out_specs=[vmem] * 5,
        compiler_params=params,
    )(me, key_rows, value_rows)

    near = range(1, count - 1, 2)
    x1r = lax.ppermute(
        x1s, "ctx", [(i, i + 1) for i in near] + [(i + 1, i) for i in near]
    )
    x2r = lax.ppermute(
        x2s,
        "ctx",
        [(i, i + 3) for i in range(0, count - 3, 2)] + [(i, i - 3) for i in range(3, count, 2)],
    )
    flow_spans = far_flows(count)
    yrs = [lax.ppermute(ys, "ctx", flow_pairs(shifts, count)) for shifts in flow_spans]
    mates = [(i, i ^ 1) for i in range(count)]
    i1r = lax.ppermute(i1s, "ctx", mates)

    def head(rows, base=0):
        return pl.BlockSpec((rows, head_size), lambda h, *_: (0, base + h))

    acc, peak, total = pl.pallas_call(
        local_kernel,
        name="local",
        grid=(HEADS,),
        out_shape=[shape(token_rows, width, jnp.float32)] * 3,
        in_specs=[head(token_rows)] * 3 + [head(token_rows // 2), head(token_rows // 2, HEADS)],
        out_specs=[head(token_rows)] * 3,
        compiler_params=params,
    )(query_rows, key_rows, value_rows, l1, l1)

    share_rows, own_rows = 384 + 64 * len(yrs), 128 + 64 * len(yrs)
    xt, i2s, own = pl.pallas_call(
        share_kernel,
        name="share",
        out_shape=[shape(TABLE_ROWS), shape(share_rows), shape(own_rows)],
        in_specs=[smem] + [vmem] * (2 + len(yrs)),
        out_specs=[vmem] * 3,
        compiler_params=params,
    )(me, x1r, x2r, *yrs)
    i2r = lax.ppermute(i2s, "ctx", mates)

    tables = []
    specs = []
    for table in (xt, i1r, i2r, own):
        tables += [table, table]
        specs += [head(table.shape[0]), head(table.shape[0], HEADS)]
    return pl.pallas_call(
        functools.partial(remote_kernel, flow_spans, count),
        name="remote",
        grid=(HEADS,),
        out_shape=shape(token_rows, width),
        in_specs=[smem, head(token_rows)] + specs + [head(token_rows)] * 3,
        out_specs=head(token_rows),
        compiler_params=params,
    )(me, query_rows, *tables, acc, peak, total)


def solution(mesh):
    spec = P(("dp", "ctx"), None)
    return jax.shard_map(
        on_device, mesh=mesh, in_specs=(spec, spec, spec), out_specs=spec, check_vma=False
    )
```

profile of v0, /device:TPU:0, one launch (start us, length us, event | category | flops | bytes accessed | tf_op | source)
XLA Modules:
  0.0 82.9 jit_solution(6525940121643942094)
XLA Ops:
  0.0 5.5 %pool.1 = (bf16[576,1024]{1,0:T(8,128)(2,1)}, bf16[896,1024]{1,0:T(8,128)(2,1)}, bf16[192,1024]{1,0:T(8,128)(2,1)}, bf16[192,1024]{1,0:T(8,128)(2,1)}, bf16[512,1024]{1,0:T(8,128)(2,1)}) custom-call(s32[1]{0:T(128)} %bitcast.dev_ref, bf16[1024,512]{1,0:T(8,128)(2,1)} %k_ref.3, bf16[1024,512]{1,0:T(8,128)(2,1)} %v_ref.3), custom_call_target="tpu_custom_call" | custom-call | tf_op jit(solution)/shard_map/pool/pallas_call | solution.py:272
  5.5 0.7 collective-permute-start
  6.3 4.3 %collective-permute-start.4 = (bf16[896,1024]{1,0:T(8,128)(2,1)}, bf16[896,1024]{1,0:T(8,128)(2,1)S(1)}, u32[]{:S(2)}, u32[]{:S(2)}) collective-permute-start(bf16[896,1024]{1,0:T(8,128)(2,1)} %get-tuple-element.20), channel_id=1, source_target_pairs={{0,4},{4,0},{8,12},{12,8},{16,20},{20,16},{24,28},{28,24},{1,5},{5... | collective-permute-start | bytes 5505032 | tf_op jit(solution)/shard_map/ppermute | solution.py:295
  10.6 3.0 %collective-permute-start.1 = (bf16[192,1024]{1,0:T(8,128)(2,1)}, bf16[192,1024]{1,0:T(8,128)(2,1)S(1)}, u32[]{:S(2)}, u32[]{:S(2)}) collective-permute-start(bf16[192,1024]{1,0:T(8,128)(2,1)} %get-tuple-element.17), channel_id=1, source_target_pairs={{0,12},{8,20},{16,28},{12,0},{20,8},{28,16},{1,13},{9,21},{17,29},... | collective-permute-start | bytes 1179656 | tf_op jit(solution)/shard_map/ppermute | solution.py:287
  13.6 1.9 %collective-permute-start.3 = (bf16[192,1024]{1,0:T(8,128)(2,1)}, bf16[192,1024]{1,0:T(8,128)(2,1)S(1)}, u32[]{:S(2)}, u32[]{:S(2)}) collective-permute-start(bf16[192,1024]{1,0:T(8,128)(2,1)} %get-tuple-element.18), channel_id=1, source_target_pairs={{24,0},{28,4},{0,24},{4,28},{25,1},{29,5},{1,25},{5,29},{26,2},{30... | collective-permute-start | bytes 1179656 | tf_op jit(solution)/shard_map/ppermute | solution.py:293
  15.5 0.1 collective-permute-start.2
  15.6 30.2 %collective-permute-done.1.x2_ref = bf16[192,1024]{1,0:T(8,128)(2,1)S(1)} collective-permute-done((bf16[192,1024]{1,0:T(8,128)(2,1)}, bf16[192,1024]{1,0:T(8,128)(2,1)S(1)}, u32[]{:S(2)}, u32[]{:S(2)}) %collective-permute-start.1) | collective-permute-done | bytes 393248 | tf_op jit(solution)/shard_map/ppermute | solution.py:287
  45.8 0.0 collective-permute-done.3.refs_1_
  45.8 0.0 collective-permute-done.2.refs_0_
  45.8 0.0 copy-start.5
  45.9 0.0 collective-permute-done.x1_ref
  45.9 0.7 copy-done.3
  46.6 0.1 copy-done.4
  46.7 0.1 copy-done.5
  46.9 1.0 %copy-done.2 = bf16[576,1024]{1,0:T(8,128)(2,1)} copy-done((bf16[576,1024]{1,0:T(8,128)(2,1)}, bf16[576,1024]{1,0:T(8,128)(2,1)S(1)}, u32[]{:S(2)}) %copy-start.2) | copy-done | bytes 1179672
  47.9 4.3 %share.1 = (bf16[896,1024]{1,0:T(8,128)(2,1)}, bf16[512,1024]{1,0:T(8,128)(2,1)}, bf16[256,1024]{1,0:T(8,128)(2,1)}) custom-call(s32[1]{0:T(128)} %bitcast.dev_ref, bf16[576,1024]{1,0:T(8,128)(2,1)} %copy-done.2, bf16[192,1024]{1,0:T(8,128)(2,1)} %copy-done.3, bf16[192,1024]{1,0:T(8,128)(2,1)} %copy-done.5, bf16[192,1024]{1,0:T(8,128)(2,1)} %copy-done.4), custom_call_target="tpu_custom_call" | custom-call | tf_op jit(solution)/shard_map/share/pallas_call | solution.py:311
  52.2 0.0 collective-permute-start.5
  52.2 9.5 %local.1 = (f32[1024,512]{1,0:T(8,128)}, f32[1024,512]{1,0:T(8,128)}, f32[1024,512]{1,0:T(8,128)}) custom-call(bf16[1024,512]{1,0:T(8,128)(2,1)} %q_ref.3, bf16[1024,512]{1,0:T(8,128)(2,1)} %k_ref.3, bf16[1024,512]{1,0:T(8,128)(2,1)} %v_ref.3, bf16[512,1024]{1,0:T(8,128)(2,1)} %get-tuple-element.23.l1k_ref.l1v_ref, ...), custom_call_target="tpu_custom_call" | custom-call | tf_op jit(solution)/shard_map/local/pallas_call | solution.py:300
  61.6 0.0 collective-permute-done.4.refs_2_.refs_3_
  61.7 0.0 collective-permute-done.5.refs_4_.refs_5_
  61.7 0.0 copy-start.1
  61.7 1.2 %copy-done = bf16[896,1024]{1,0:T(8,128)(2,1)} copy-done((bf16[896,1024]{1,0:T(8,128)(2,1)}, bf16[896,1024]{1,0:T(8,128)(2,1)S(1)}, u32[]{:S(2)}) %copy-start) | copy-done | bytes 1835032
  62.9 0.3 copy-done.1
  63.2 19.7 %remote.1 = bf16[1024,512]{1,0:T(8,128)(2,1)} custom-call(s32[1]{0:T(128)} %bitcast.dev_ref, bf16[1024,512]{1,0:T(8,128)(2,1)} %q_ref.3, bf16[896,1024]{1,0:T(8,128)(2,1)} %get-tuple-element.19.refs_0_.refs_1_, bf16[896,1024]{1,0:T(8,128)(2,1)} %get-tuple-element.19.refs_0_.refs_1_, bf16[896,1024]{1,0:T(8,128)(2,1)} %copy-done, bf16[896,1024]{1,0:T(8,128)(2,1)} %copy-done, ...), custom_call_target="tpu_custom_call" | custom-call | tf_op jit(solution)/shard_map/remote/pallas_call | solution.py:326
  (4 shorter events, 0.0 us)
Async XLA Ops:
  5.5 40.3 %collective-permute-start = (bf16[576,1024]{1,0:T(8,128)(2,1)}, bf16[576,1024]{1,0:T(8,128)(2,1)S(1)}, u32[]{:S(2)}, u32[]{:S(2)}) collective-permute-start(bf16[576,1024]{1,0:T(8,128)(2,1)} %get-tuple-element.16), channel_id=1, source_target_pairs={{4,8},{12,16},{20,24},{8,4},{16,12},{24,20},{5,9},{13,17},{21,25},... | collective-permute-start | bytes 3538952 | tf_op jit(solution)/shard_map/ppermute | solution.py:284
  6.3 55.4 %collective-permute-start.4 = (bf16[896,1024]{1,0:T(8,128)(2,1)}, bf16[896,1024]{1,0:T(8,128)(2,1)S(1)}, u32[]{:S(2)}, u32[]{:S(2)}) collective-permute-start(bf16[896,1024]{1,0:T(8,128)(2,1)} %get-tuple-element.20), channel_id=1, source_target_pairs={{0,4},{4,0},{8,12},{12,8},{16,20},{20,16},{24,28},{28,24},{1,5},{5... | collective-permute-start | bytes 5505032 | tf_op jit(solution)/shard_map/ppermute | solution.py:295
  10.6 35.3 %collective-permute-start.1 = (bf16[192,1024]{1,0:T(8,128)(2,1)}, bf16[192,1024]{1,0:T(8,128)(2,1)S(1)}, u32[]{:S(2)}, u32[]{:S(2)}) collective-permute-start(bf16[192,1024]{1,0:T(8,128)(2,1)} %get-tuple-element.17), channel_id=1, source_target_pairs={{0,12},{8,20},{16,28},{12,0},{20,8},{28,16},{1,13},{9,21},{17,29},... | collective-permute-start | bytes 1179656 | tf_op jit(solution)/shard_map/ppermute | solution.py:287
  13.6 32.2 %collective-permute-start.3 = (bf16[192,1024]{1,0:T(8,128)(2,1)}, bf16[192,1024]{1,0:T(8,128)(2,1)S(1)}, u32[]{:S(2)}, u32[]{:S(2)}) collective-permute-start(bf16[192,1024]{1,0:T(8,128)(2,1)} %get-tuple-element.18), channel_id=1, source_target_pairs={{24,0},{28,4},{0,24},{4,28},{25,1},{29,5},{1,25},{5,29},{26,2},{30... | collective-permute-start | bytes 1179656 | tf_op jit(solution)/shard_map/ppermute | solution.py:293
  15.5 30.3 %collective-permute-start.2 = (bf16[192,1024]{1,0:T(8,128)(2,1)}, bf16[192,1024]{1,0:T(8,128)(2,1)S(1)}, u32[]{:S(2)}, u32[]{:S(2)}) collective-permute-start(bf16[192,1024]{1,0:T(8,128)(2,1)} %get-tuple-element.18), channel_id=1, source_target_pairs={{16,0},{20,4},{24,8},{28,12},{0,16},{4,20},{8,24},{12,28},{17,1},{... | collective-permute-start | bytes 1179656 | tf_op jit(solution)/shard_map/ppermute | solution.py:293
  45.8 0.8 copy-start.3
  45.8 0.9 %copy-start.4 = (bf16[192,1024]{1,0:T(8,128)(2,1)}, bf16[192,1024]{1,0:T(8,128)(2,1)S(1)}, u32[]{:S(2)}) copy-start(bf16[192,1024]{1,0:T(8,128)(2,1)S(1)} %collective-permute-done.3.refs_1_) | copy-start | bytes 1179652
  45.8 1.0 %copy-start.5 = (bf16[192,1024]{1,0:T(8,128)(2,1)}, bf16[192,1024]{1,0:T(8,128)(2,1)S(1)}, u32[]{:S(2)}) copy-start(bf16[192,1024]{1,0:T(8,128)(2,1)S(1)} %collective-permute-done.2.refs_0_) | copy-start | bytes 1179652
  46.9 1.0 %copy-start.2 = (bf16[576,1024]{1,0:T(8,128)(2,1)}, bf16[576,1024]{1,0:T(8,128)(2,1)S(1)}, u32[]{:S(2)}) copy-start(bf16[576,1024]{1,0:T(8,128)(2,1)S(1)} %collective-permute-done.x1_ref) | copy-start | bytes 3538948
  52.2 9.5 %collective-permute-start.5 = (bf16[512,1024]{1,0:T(8,128)(2,1)}, bf16[512,1024]{1,0:T(8,128)(2,1)S(1)}, u32[]{:S(2)}, u32[]{:S(2)}) collective-permute-start(bf16[512,1024]{1,0:T(8,128)(2,1)} %get-tuple-element.21), channel_id=1, source_target_pairs={{0,4},{4,0},{8,12},{12,8},{16,20},{20,16},{24,28},{28,24},{1,5},{5... | collective-permute-start | bytes 3145736 | tf_op jit(solution)/shard_map/ppermute | solution.py:319
  61.7 1.3 %copy-start = (bf16[896,1024]{1,0:T(8,128)(2,1)}, bf16[896,1024]{1,0:T(8,128)(2,1)S(1)}, u32[]{:S(2)}) copy-start(bf16[896,1024]{1,0:T(8,128)(2,1)S(1)} %collective-permute-done.4.refs_2_.refs_3_) | copy-start | bytes 5505028
  61.7 1.6 %copy-start.1 = (bf16[512,1024]{1,0:T(8,128)(2,1)}, bf16[512,1024]{1,0:T(8,128)(2,1)S(1)}, u32[]{:S(2)}) copy-start(bf16[512,1024]{1,0:T(8,128)(2,1)S(1)} %collective-permute-done.5.refs_4_.refs_5_) | copy-start | bytes 3145732
where the time goes:
time: 83.3 us; the launch traced here: 82.9 us
  Pallas kernels  39 us (47%)
  waiting for transfers between devices  30.2 us (36%)
  starting transfers between devices  10 us (12%)
  local copies, waits for them, and re-layouts  3.59 us (4%)
    ppermute x1, waiting for transfers between devices, on_device(): lax.ppermute(x2s, 'ctx', [(i, i + 3) for i in range(0, count - 3, 2)] + [...  30.2 us
    pallas_call x1, Pallas kernels, on_device(): pl.pallas_call(functools.partial(remote_kernel, flow_spans, count), name=...  19.7 us
    pallas_call x1, Pallas kernels, on_device(): pl.pallas_call(local_kernel, name='local', grid=(HEADS,), out_shape=[shap...  9.47 us
    pallas_call x1, Pallas kernels, on_device(): pl.pallas_call(pool_kernel, name='pool', out_shape=[shape(RIM_ROWS), shap...  5.54 us
    ppermute x1, starting transfers between devices, on_device(): i1r = lax.ppermute(i1s, 'ctx', mates)  4.29 us
    pallas_call x1, Pallas kernels, on_device(): pl.pallas_call(share_kernel, name='share', out_shape=[shape(TABLE_ROWS),...  4.29 us
    unnamed x12, local copies, waits for them, and re-layouts  3.59 us
    ppermute x1, starting transfers between devices, on_device(): lax.ppermute(x2s, 'ctx', [(i, i + 3) for i in range(0, count - 3, 2)] + [...  3.02 us
  transfers between devices with their start and end apart: 6, of which 1 were waited for; matrix products, arithmetic and copies ran while one was open for 0% of the time, Pallas kernels for 17%

commit v1 on v0

--- a/solution.py
+++ b/solution.py
@@ -3,6 +3,8 @@
 
 import jax
 import jax.numpy as jnp
+import ml_dtypes
+import numpy as np
 from jax import lax
 from jax.experimental import pallas as pl
 from jax.experimental.pallas import tpu as pltpu
@@ -110,44 +112,72 @@
         own_ref[64:128, :] = x2_ref[128:192, :]
 
 
+def offset_lanes(level, valid, scale):
+    terms = []
+    rest = level / scale
+    for _ in range(3):
+        term = float(np.float32(rest).astype(ml_dtypes.bfloat16))
+        terms.append(term)
+        rest -= term
+    if valid is not None:
+        terms = [jnp.where(valid, t, h) for t, h in zip(terms, (HIDDEN, 0.0, 0.0))]
+    lane = lax.broadcasted_iota(jnp.int32, (128, 128), 1)
+    lanes = jnp.zeros((128, 128), jnp.float32)
+    for at, term in enumerate(terms):
+        lanes = jnp.where(lane == at, term, lanes)
+    return lanes.astype(jnp.bfloat16)
+
+
+def chunks_of(segments):
+    chunks = [[]]
+    room = 256
+    for k_ref, v_ref, start, count, lanes in segments:
+        while count:
+            take = min(count, room, 128)
+            chunks[-1].append((k_ref, v_ref, start, take, lanes))
+            start, count, room = start + take, count - take, room - take
+            if not room:
+                chunks.append([])
+                room = 256
+    return [chunk for chunk in chunks if chunk]
+
+
 def attend(query, segments, scale, before):
     rows = query.shape[0]
+    lane = lax.broadcasted_iota(jnp.int32, query.shape, 1)
+    query = jnp.concatenate([query, jnp.where(lane < 3, 1.0, 0.0).astype(query.dtype)], axis=1)
+    chunks = chunks_of(segments)
     scores = []
     peak = None
-    for k_ref, _, start, count, offset in segments:
+    for chunk in chunks:
+        keys = jnp.concatenate(
+            [
+                jnp.concatenate([k_ref[start : start + count, :], lanes[0:count]], axis=1)
+                for k_ref, _, start, count, lanes in chunk
+            ],
+            axis=0,
+        )
         score = lax.dot_general(
-            query,
-            k_ref[start : start + count, :],
-            (((1,), (1,)), ((), ())),
-            preferred_element_type=jnp.float32,
+            query, keys, (((1,), (1,)), ((), ())), preferred_element_type=jnp.float32
         )
         scores.append(score)
-        top = score[:, 0:128]
-        for col in range(128, count, 128):
-            top = jnp.maximum(top, score[:, col : col + 128])
-        if count < 128:
-            top = jnp.max(score, axis=1, keepdims=True)
-        top = top * scale + offset
-        if top.shape[1] < 128:
-            top = jnp.broadcast_to(top, (rows, 128))
-        peak = top if peak is None else jnp.maximum(peak, top)
-    peak = jnp.broadcast_to(jnp.max(peak, axis=1, keepdims=True), (rows, 128))
+        for col in range(0, keys.shape[0], 128):
+            top = score[:, col : col + 128]
+            peak = top if peak is None else jnp.maximum(peak, top)
+    peak = jnp.max(peak, axis=1, keepdims=True) * scale
     if before is not None:
-        peak = jnp.maximum(peak, before)
+        peak = jnp.maximum(jnp.broadcast_to(peak, before.shape), before)
+        lifted = peak[:, 0:1]
+    else:
+        lifted = peak
     out = None
-    for (_, v_ref, start, count, offset), score in zip(segments, scores):
-        lifted = peak - offset
-        weights = []
-        for col in range(0, count, 128):
-            piece = score[:, col : min(col + 128, count)]
-            weights.append(jnp.exp2(piece * scale - lifted[:, : piece.shape[1]]))
-        weight = jnp.concatenate(weights, axis=1) if len(weights) > 1 else weights[0]
-        table = jnp.concatenate(
-            [v_ref[start : start + count, :], jnp.ones((count, 128), jnp.bfloat16)], axis=1
+    for chunk, score in zip(chunks, scores):
+        weight = jnp.exp2(score * scale - lifted).astype(jnp.bfloat16)
+        values = jnp.concatenate(
+            [v_ref[start : start + count, :] for _, v_ref, start, count, _ in chunk], axis=0
         )
-        part = jnp.dot(
-            weight.astype(jnp.bfloat16), table, preferred_element_type=jnp.float32
-        )
+        table = jnp.concatenate([values, jnp.ones((values.shape[0], 128), jnp.bfloat16)], axis=1)
+        part = jnp.dot(weight, table, preferred_element_type=jnp.float32)
         out = part if out is None else out + part
     return peak, out[:, 0:128], out[:, 128:256]
 
@@ -156,33 +186,59 @@
     return math.log2(math.e) / math.sqrt(head_size)
 
 
-def local_kernel(q_ref, k_ref, v_ref, l1k_ref, l1v_ref, acc_ref, peak_ref, total_ref):
+def near_kernel(count, dev_ref, q_ref, k_ref, v_ref, l1k, l1v, mk, mv, acc_ref, peak_ref, total_ref):
     scale = base_two_scale(q_ref.shape[1])
-    own = {0: ((256, 256),), 1: (), 2: ((0, 128),), 3: ((0, 256),)}
-    for block in range(BLOCKS):
-        low, high = max(block - 1, 0), min(block + 2, BLOCKS)
-        segments = [(k_ref, v_ref, low * LEAF, (high - low) * LEAF, 0.0)]
-        for start, count in own[block]:
-            segments.append((l1k_ref, l1v_ref, start, count, 1.0))
-        here = slice(block * LEAF, (block + 1) * LEAF)
-        peak, acc, total = attend(q_ref[here, :], segments, scale, None)
-        acc_ref[here, :] = acc
-        peak_ref[here, :] = peak
-        total_ref[here, :] = total
-
-
-def remote_kernel(flow_spans, count, dev_ref, q_ref, *refs):
-    (xtk, xtv, i1k, i1v, i2k, i2v, ownk, ownv, acc_ref, peak_ref, total_ref, out_ref) = refs
+    zero = offset_lanes(0, None, scale)
+    one = offset_lanes(1, None, scale)
+    two = offset_lanes(2, None, scale)
+    own = ((256, 256), None, (0, 128), (0, 256))
+
+    def run(odd):
+        if odd:
+            mate = (
+                [(mk, mv, 0, 256, zero), (mk, mv, L1_AT, 128, one), (mk, mv, L2_AT, 128, two)],
+                [(mk, mv, L1_AT, 256, one), (mk, mv, L2_AT, 128, two)],
+                [(mk, mv, L2_AT, 256, two)],
+                [(mk, mv, L2_AT, 256, two)],
+            )
+        else:
+            mate = (
+                [(mk, mv, L2_AT, 256, two)],
+                [(mk, mv, L1_AT, 128, one), (mk, mv, L2_AT, 256, two)],
+                [(mk, mv, L1_AT, 256, one)],
+                [(mk, mv, 0, 256, zero), (mk, mv, L1_AT + 256, 128, one)],
+            )
+        for block in range(BLOCKS):
+            low, high = max(block - 1, 0), min(block + 2, BLOCKS)
+            segments = [(k_ref, v_ref, low * LEAF, (high - low) * LEAF, zero)]
+            if own[block]:
+                segments.append((l1k, l1v, own[block][0], own[block][1], one))
+            here = slice(block * LEAF, (block + 1) * LEAF)
+            peak, acc, total = attend(q_ref[here, :], segments + mate[block], scale, None)
+            acc_ref[here, :] = acc
+            peak_ref[here, :] = jnp.broadcast_to(peak, acc.shape)
+            total_ref[here, :] = total
+
+    @pl.when(dev_ref[0] % 2 == 1)
+    def _():
+        run(True)
+
+    @pl.when(dev_ref[0] % 2 == 0)
+    def _():
+        run(False)
+
+
+def far_kernel(flow_spans, count, dev_ref, q_ref, *refs):
+    (xk, xv, i2k, i2v, ownk, ownv, acc_ref, peak_ref, total_ref, out_ref) = refs
     scale = base_two_scale(q_ref.shape[1])
     me = dev_ref[0]
     chip = me // 2
     chips = count // 2
 
-    def offset(level, valid):
-        return jnp.where(valid, float(level), HIDDEN).astype(jnp.float32)
-
-    left, right = me >= 1, me < count - 1
-    flows = []
+    def lanes(level, valid):
+        return offset_lanes(level, valid, scale)
+
+    fours = []
     for shifts in flow_spans:
         valid = False
         for shift in shifts:
@@ -193,35 +249,41 @@
             if shift == 6:
                 here = here & (chip % 2 == 1)
             valid = here | valid
-        flows.append(valid)
-
-    def run(odd, lk, lv, rk, rv):
+        fours.append(lanes(4, valid))
+
+    def run(odd):
+        near = (me < count - 1) if odd else (me >= 1)
         a_ok = (me - 2 >= 0) if odd else (me + 2 < count)
         b_ok = (me + 3 < count) if odd else (me - 2 >= 0)
         c_ok = (me - 3 >= 0) if odd else (me + 3 < count)
         coarse = [
-            (i2k, i2v, 128, 128, offset(3, a_ok)),
-            (i2k, i2v, 256, 128, offset(3, b_ok)),
-            (ownk, ownv, 0, 128, offset(3, c_ok)),
+            (i2k, i2v, 128, 128, lanes(3, a_ok)),
+            (i2k, i2v, 256, 128, lanes(3, b_ok)),
+            (ownk, ownv, 0, 128, lanes(3, c_ok)),
         ]
-        for slot, valid in enumerate(flows):
-            coarse.append((i2k, i2v, 384 + 64 * slot, 64, offset(4, valid)))
-            coarse.append((ownk, ownv, 128 + 64 * slot, 64, offset(4, valid)))
-        second = (
-            [(lk, lv, L2_AT, 128, offset(2, left)), (rk, rv, L2_AT, 256, offset(2, right))],
-            [(lk, lv, L2_AT, 256, offset(2, left)), (i2k, i2v, 0, 128, offset(2, me + 2 < count))],
-        )
-        edges = (
-            [(lk, lv, 0, 256, offset(0, left)), (lk, lv, L1_AT, 128, offset(1, left))],
-            [(lk, lv, L1_AT, 256, offset(1, left)), (rk, rv, L1_AT, 128, offset(1, right))],
-            [(rk, rv, L1_AT, 256, offset(1, right))],
-            [(rk, rv, 0, 256, offset(0, right)), (rk, rv, L1_AT + 256, 128, offset(1, right))],
-        )
+        for slot, four in enumerate(fours):
+            coarse.append((i2k, i2v, 384 + 64 * slot, 64, four))
+            coarse.append((ownk, ownv, 128 + 64 * slot, 64, four))
+        zero, one, two = (lanes(level, near) for level in range(3))
+        skip = (i2k, i2v, 0, 128, lanes(2, me + 2 < count))
+        if odd:
+            rim = (
+                [(xk, xv, L2_AT, 256, two)],
+                [(xk, xv, L1_AT, 128, one), (xk, xv, L2_AT, 256, two)],
+                [(xk, xv, L1_AT, 256, one), skip],
+                [(xk, xv, 0, 256, zero), (xk, xv, L1_AT + 256, 128, one), skip],
+            )
+        else:
+            rim = (
+                [(xk, xv, 0, 256, zero), (xk, xv, L1_AT, 128, one), (xk, xv, L2_AT, 128, two)],
+                [(xk, xv, L1_AT, 256, one), (xk, xv, L2_AT, 128, two)],
+                [(xk, xv, L2_AT, 256, two), skip],
+                [(xk, xv, L2_AT, 256, two), skip],
+            )
         for block in range(BLOCKS):
             here = slice(block * LEAF, (block + 1) * LEAF)
-            segments = edges[block] + second[block // 2] + coarse
             before = peak_ref[here, :]
-            peak, acc, total = attend(q_ref[here, :], segments, scale, before)
+            peak, acc, total = attend(q_ref[here, :], rim[block] + coarse, scale, before)
             factor = jnp.exp2(before - peak)
             acc = acc_ref[here, :] * factor + acc
             total = total_ref[here, :] * factor + total
@@ -229,11 +291,11 @@
 
     @pl.when(me % 2 == 1)
     def _():
-        run(True, i1k, i1v, xtk, xtv)
+        run(True)
 
     @pl.when(me % 2 == 0)
     def _():
-        run(False, xtk, xtv, i1k, i1v)
+        run(False)
 
 
 def flow_pairs(shifts, count):
@@ -267,7 +329,7 @@
 
     smem = pl.BlockSpec(memory_space=pltpu.SMEM)
     vmem = pl.BlockSpec(memory_space=pltpu.VMEM)
-    params = pltpu.CompilerParams(vmem_limit_bytes=56 << 20)
+    params = pltpu.CompilerParams(vmem_limit_bytes=63 << 20)
 
     x1s, i1s, x2s, ys, l1 = pl.pallas_call(
         pool_kernel,
@@ -297,16 +359,29 @@
     def head(rows, base=0):
         return pl.BlockSpec((rows, head_size), lambda h, *_: (0, base + h))
 
+    def cost(keys, rows):
+        pairs = token_rows * keys * HEADS
+        return pl.CostEstimate(
+            flops=4 * pairs * head_size,
+            transcendentals=pairs,
+            bytes_accessed=rows * 4 * width,
+        )
+
     acc, peak, total = pl.pallas_call(
-        local_kernel,
-        name="local",
+        functools.partial(near_kernel, count),
+        name="near",
         grid=(HEADS,),
         out_shape=[shape(token_rows, width, jnp.float32)] * 3,
-        in_specs=[head(token_rows)] * 3 + [head(token_rows // 2), head(token_rows // 2, HEADS)],
+        in_specs=[smem]
+        + [head(token_rows)] * 3
+        + [head(token_rows // 2), head(token_rows // 2, HEADS)]
+        + [head(TABLE_ROWS), head(TABLE_ROWS, HEADS)],
         out_specs=[head(token_rows)] * 3,
         compiler_params=params,
-    )(query_rows, key_rows, value_rows, l1, l1)
-
+        cost_estimate=cost(1152, 6000),
+    )(me, query_rows, key_rows, value_rows, l1, l1, i1r, i1r)
+
+    x1r, x2r, yrs, acc, peak, total = lax.optimization_barrier((x1r, x2r, yrs, acc, peak, total))
     share_rows, own_rows = 384 + 64 * len(yrs), 128 + 64 * len(yrs)
     xt, i2s, own = pl.pallas_call(
         share_kernel,
@@ -320,17 +395,18 @@
 
     tables = []
     specs = []
-    for table in (xt, i1r, i2r, own):
+    for table in (xt, i2r, own):
         tables += [table, table]
         specs += [head(table.shape[0]), head(table.shape[0], HEADS)]
     return pl.pallas_call(
-        functools.partial(remote_kernel, flow_spans, count),
-        name="remote",
+        functools.partial(far_kernel, flow_spans, count),
+        name="far",
         grid=(HEADS,),
         out_shape=shape(token_rows, width),
         in_specs=[smem, head(token_rows)] + specs + [head(token_rows)] * 3,
         out_specs=head(token_rows),
         compiler_params=params,
+        cost_estimate=cost(1152, 6000),
     )(me, query_rows, *tables, acc, peak, total)
 
 

time: 83.3 us -> 65.8 us (0.79)
  waiting for transfers between devices: 30.2 us -> 21.7 us
  Pallas kernels: 39 us -> 33 us
  local copies, waits for them, and re-layouts: 3.59 us -> 0.87 us
    ppermute x1, waiting for transfers between devices: 30.2 us -> 18.7 us  [on_device(): lax.ppermute(x2s, 'ctx', [(i, i + 3) for i in range(0, count - 3, 2)] + [...]
    pallas_call x2, Pallas kernels: 29.2 us -> 23.4 us  [the longest x1 11.8 us: on_device(): pl.pallas_call(functools.partial(far_kernel, flow_spans, count), name='fa...]
    ppermute x1, starting transfers between devices: 4.29 us -> 0.44 us  [on_device(): i1r = lax.ppermute(i1s, 'ctx', mates)]
    ppermute x1, waiting for transfers between devices: 0.01 us -> 3 us  [on_device(): i2r = lax.ppermute(i2s, 'ctx', mates)]
    ppermute x1, starting transfers between devices: 3.02 us -> 5.83 us  [on_device(): lax.ppermute(x2s, 'ctx', [(i, i + 3) for i in range(0, count - 3, 2)] + [...]
    unnamed x12 -> x4, local copies, waits for them, and re-layouts: 3.59 us -> 0.87 us
    ppermute x1, starting transfers between devices: 0.72 us -> 1.69 us  [on_device(): lax.ppermute(x1s, 'ctx', [(i, i + 1) for i in near] + [(i + 1, i) for i i...]
  transfers between devices with their start and end apart: 6 -> 6, of which waited for: 1 -> 2; matrix products, arithmetic and copies ran while one was open for 0% -> 0% of each run, Pallas kernels for 17% -> 18%
where the time goes in v1:
time: 65.8 us; the launch traced here: 65.5 us
  Pallas kernels  33 us (50%)
  waiting for transfers between devices  21.7 us (33%)
  starting transfers between devices  9.96 us (15%)
  local copies, waits for them, and re-layouts  0.87 us (1%)
    ppermute x1, waiting for transfers between devices, on_device(): lax.ppermute(x2s, 'ctx', [(i, i + 3) for i in range(0, count - 3, 2)] + [...  18.7 us
    pallas_call x1, Pallas kernels, on_device(): pl.pallas_call(functools.partial(far_kernel, flow_spans, count), name='fa...  11.8 us
    pallas_call x1, Pallas kernels, on_device(): pl.pallas_call(functools.partial(near_kernel, count), name='near', grid=(...  11.6 us
    ppermute x1, starting transfers between devices, on_device(): lax.ppermute(x2s, 'ctx', [(i, i + 3) for i in range(0, count - 3, 2)] + [...  5.83 us
    pallas_call x1, Pallas kernels, on_device(): pl.pallas_call(pool_kernel, name='pool', out_shape=[shape(RIM_ROWS), shap...  5.55 us
    pallas_call x1, Pallas kernels, on_device(): pl.pallas_call(share_kernel, name='share', out_shape=[shape(TABLE_ROWS),...  4.03 us
    ppermute x1, waiting for transfers between devices, on_device(): i2r = lax.ppermute(i2s, 'ctx', mates)  3 us
    ppermute x2, starting transfers between devices, on_device(): lax.ppermute(ys, 'ctx', flow_pairs(shifts, count))  1.99 us
  transfers between devices with their start and end apart: 6, of which 2 were waited for; matrix products, arithmetic and copies ran while one was open for 0% of the time, Pallas kernels for 18%

profile of v1, /device:TPU:0, one launch (start us, length us, event | category | flops | bytes accessed | tf_op | source)
XLA Modules:
  0.0 65.5 jit_solution(2471088541097177456)
XLA Ops:
  0.0 5.6 %pool.1 = (bf16[576,1024]{1,0:T(8,128)(2,1)}, bf16[896,1024]{1,0:T(8,128)(2,1)}, bf16[192,1024]{1,0:T(8,128)(2,1)}, bf16[192,1024]{1,0:T(8,128)(2,1)}, bf16[512,1024]{1,0:T(8,128)(2,1)}) custom-call(s32[1]{0:T(128)} %bitcast.dev_ref, bf16[1024,512]{1,0:T(8,128)(2,1)} %k_ref.3, bf16[1024,512]{1,0:T(8,128)(2,1)} %v_ref.3), custom_call_target="tpu_custom_call" | custom-call | tf_op jit(solution)/shard_map/pool/pallas_call | solution.py:334
  5.6 0.4 collective-permute-start.4
  6.0 1.7 %collective-permute-start = (bf16[576,1024]{1,0:T(8,128)(2,1)}, bf16[576,1024]{1,0:T(8,128)(2,1)}, u32[]{:S(2)}, u32[]{:S(2)}) collective-permute-start(bf16[576,1024]{1,0:T(8,128)(2,1)} %get-tuple-element.23), channel_id=1, source_target_pairs={{4,8},{12,16},{20,24},{8,4},{16,12},{24,20},{5,9},{13,17},{21,25},... | collective-permute-start | bytes 3538952 | tf_op jit(solution)/shard_map/ppermute | solution.py:346
  7.7 5.8 %collective-permute-start.1 = (bf16[192,1024]{1,0:T(8,128)(2,1)}, bf16[192,1024]{1,0:T(8,128)(2,1)S(1)}, u32[]{:S(2)}, u32[]{:S(2)}) collective-permute-start(bf16[192,1024]{1,0:T(8,128)(2,1)} %get-tuple-element.24), channel_id=1, source_target_pairs={{0,12},{8,20},{16,28},{12,0},{20,8},{28,16},{1,13},{9,21},{17,29},... | collective-permute-start | bytes 1179656 | tf_op jit(solution)/shard_map/ppermute | solution.py:349
  13.5 1.9 %collective-permute-start.3 = (bf16[192,1024]{1,0:T(8,128)(2,1)}, bf16[192,1024]{1,0:T(8,128)(2,1)S(1)}, u32[]{:S(2)}, u32[]{:S(2)}) collective-permute-start(bf16[192,1024]{1,0:T(8,128)(2,1)} %get-tuple-element.25), channel_id=1, source_target_pairs={{24,0},{28,4},{0,24},{4,28},{25,1},{29,5},{1,25},{5,29},{26,2},{30... | collective-permute-start | bytes 1179656 | tf_op jit(solution)/shard_map/ppermute | solution.py:355
  15.5 0.1 collective-permute-start.2
  15.5 0.0 collective-permute-done.4.mk.mv
  15.5 11.6 %near.1 = (f32[1024,512]{1,0:T(8,128)}, f32[1024,512]{1,0:T(8,128)}, f32[1024,512]{1,0:T(8,128)}) custom-call(s32[1]{0:T(128)} %bitcast.dev_ref, bf16[1024,512]{1,0:T(8,128)(2,1)} %q_ref.3, bf16[1024,512]{1,0:T(8,128)(2,1)} %k_ref.3, bf16[1024,512]{1,0:T(8,128)(2,1)} %v_ref.3, bf16[512,1024]{1,0:T(8,128)(2,1)} %get-tuple-element.26.l1k.l1v, ...), custom_call_target="tpu_custom_call" | custom-call | flops 2415919104 | bytes 12288000 | tf_op jit(solution)/shard_map/near/pallas_call | solution.py:370
  27.2 18.7 %collective-permute-done.1.x2_ref = bf16[192,1024]{1,0:T(8,128)(2,1)S(1)} collective-permute-done((bf16[192,1024]{1,0:T(8,128)(2,1)}, bf16[192,1024]{1,0:T(8,128)(2,1)S(1)}, u32[]{:S(2)}, u32[]{:S(2)}) %collective-permute-start.1) | collective-permute-done | bytes 393248 | tf_op jit(solution)/shard_map/ppermute | solution.py:349
  45.8 0.0 copy-start
  45.8 0.0 collective-permute-done.3.refs_1_
  45.9 0.0 copy-start.1
  45.9 0.0 collective-permute-done.2.refs_0_
  45.9 0.0 collective-permute-done.x1_ref
  45.9 0.7 %copy-done = bf16[192,1024]{1,0:T(8,128)(2,1)} copy-done((bf16[192,1024]{1,0:T(8,128)(2,1)}, bf16[192,1024]{1,0:T(8,128)(2,1)S(1)}, u32[]{:S(2)}) %copy-start) | copy-done | bytes 393240
  46.6 0.1 copy-done.1
  46.7 4.0 %share.1 = (bf16[896,1024]{1,0:T(8,128)(2,1)}, bf16[512,1024]{1,0:T(8,128)(2,1)}, bf16[256,1024]{1,0:T(8,128)(2,1)}) custom-call(s32[1]{0:T(128)} %bitcast.dev_ref, bf16[576,1024]{1,0:T(8,128)(2,1)} %collective-permute-done.x1_ref, bf16[192,1024]{1,0:T(8,128)(2,1)} %copy-done, bf16[192,1024]{1,0:T(8,128)(2,1)} %collective-permute-done.2.refs_0_, ...), custom_call_target="tpu_custom_call" | custom-call | tf_op jit(solution)/shard_map/share/pallas_call | solution.py:386
  50.8 0.0 collective-permute-start.5
  50.8 3.0 %collective-permute-done.5.refs_2_.refs_3_ = bf16[512,1024]{1,0:T(8,128)(2,1)} collective-permute-done((bf16[512,1024]{1,0:T(8,128)(2,1)}, bf16[512,1024]{1,0:T(8,128)(2,1)}, u32[]{:S(2)}, u32[]{:S(2)}) %collective-permute-start.5) | collective-permute-done | bytes 1048608 | tf_op jit(solution)/shard_map/ppermute | solution.py:394
  53.8 11.8 %far.1 = bf16[1024,512]{1,0:T(8,128)(2,1)} custom-call(s32[1]{0:T(128)} %bitcast.dev_ref, bf16[1024,512]{1,0:T(8,128)(2,1)} %q_ref.3, bf16[896,1024]{1,0:T(8,128)(2,1)} %get-tuple-element.35.refs_0_.refs_1_, bf16[896,1024]{1,0:T(8,128)(2,1)} %get-tuple-element.35.refs_0_.refs_1_, bf16[512,1024]{1,0:T(8,128)(2,1)} %collective-permute-done.5.refs_2_.refs_3_, ...), custom_call_target="tpu_custom_call" | custom-call | flops 2415919104 | bytes 12288000 | tf_op jit(solution)/shard_map/far/pallas_call | solution.py:401
Async XLA Ops:
  5.6 10.0 %collective-permute-start.4 = (bf16[896,1024]{1,0:T(8,128)(2,1)}, bf16[896,1024]{1,0:T(8,128)(2,1)}, u32[]{:S(2)}, u32[]{:S(2)}) collective-permute-start(bf16[896,1024]{1,0:T(8,128)(2,1)} %get-tuple-element.27), channel_id=1, source_target_pairs={{0,4},{4,0},{8,12},{12,8},{16,20},{20,16},{24,28},{28,24},{1,5},{5... | collective-permute-start | bytes 5505032 | tf_op jit(solution)/shard_map/ppermute | solution.py:357
  6.0 39.9 %collective-permute-start = (bf16[576,1024]{1,0:T(8,128)(2,1)}, bf16[576,1024]{1,0:T(8,128)(2,1)}, u32[]{:S(2)}, u32[]{:S(2)}) collective-permute-start(bf16[576,1024]{1,0:T(8,128)(2,1)} %get-tuple-element.23), channel_id=1, source_target_pairs={{4,8},{12,16},{20,24},{8,4},{16,12},{24,20},{5,9},{13,17},{21,25},... | collective-permute-start | bytes 3538952 | tf_op jit(solution)/shard_map/ppermute | solution.py:346
  7.7 38.2 %collective-permute-start.1 = (bf16[192,1024]{1,0:T(8,128)(2,1)}, bf16[192,1024]{1,0:T(8,128)(2,1)S(1)}, u32[]{:S(2)}, u32[]{:S(2)}) collective-permute-start(bf16[192,1024]{1,0:T(8,128)(2,1)} %get-tuple-element.24), channel_id=1, source_target_pairs={{0,12},{8,20},{16,28},{12,0},{20,8},{28,16},{1,13},{9,21},{17,29},... | collective-permute-start | bytes 1179656 | tf_op jit(solution)/shard_map/ppermute | solution.py:349
  13.5 32.3 %collective-permute-start.3 = (bf16[192,1024]{1,0:T(8,128)(2,1)}, bf16[192,1024]{1,0:T(8,128)(2,1)S(1)}, u32[]{:S(2)}, u32[]{:S(2)}) collective-permute-start(bf16[192,1024]{1,0:T(8,128)(2,1)} %get-tuple-element.25), channel_id=1, source_target_pairs={{24,0},{28,4},{0,24},{4,28},{25,1},{29,5},{1,25},{5,29},{26,2},{30... | collective-permute-start | bytes 1179656 | tf_op jit(solution)/shard_map/ppermute | solution.py:355
  15.5 30.4 %collective-permute-start.2 = (bf16[192,1024]{1,0:T(8,128)(2,1)}, bf16[192,1024]{1,0:T(8,128)(2,1)}, u32[]{:S(2)}, u32[]{:S(2)}) collective-permute-start(bf16[192,1024]{1,0:T(8,128)(2,1)} %get-tuple-element.25), channel_id=1, source_target_pairs={{16,0},{20,4},{24,8},{28,12},{0,16},{4,20},{8,24},{12,28},{17,1},{... | collective-permute-start | bytes 1179656 | tf_op jit(solution)/shard_map/ppermute | solution.py:355
  45.8 0.8 %copy-start = (bf16[192,1024]{1,0:T(8,128)(2,1)}, bf16[192,1024]{1,0:T(8,128)(2,1)S(1)}, u32[]{:S(2)}) copy-start(bf16[192,1024]{1,0:T(8,128)(2,1)S(1)} %collective-permute-done.1.x2_ref) | copy-start | bytes 1179652
  45.9 0.9 %copy-start.1 = (bf16[192,1024]{1,0:T(8,128)(2,1)}, bf16[192,1024]{1,0:T(8,128)(2,1)S(1)}, u32[]{:S(2)}) copy-start(bf16[192,1024]{1,0:T(8,128)(2,1)S(1)} %collective-permute-done.3.refs_1_) | copy-start | bytes 1179652
  50.8 3.0 %collective-permute-start.5 = (bf16[512,1024]{1,0:T(8,128)(2,1)}, bf16[512,1024]{1,0:T(8,128)(2,1)}, u32[]{:S(2)}, u32[]{:S(2)}) collective-permute-start(bf16[512,1024]{1,0:T(8,128)(2,1)} %get-tuple-element.36), channel_id=1, source_target_pairs={{0,4},{4,0},{8,12},{12,8},{16,20},{20,16},{24,28},{28,24},{1,5},{5... | collective-permute-start | bytes 3145736 | tf_op jit(solution)/shard_map/ppermute | solution.py:394

commit v2 on v1

v2 whole, which is shorter than its diff:
```python
import functools
import math

import jax
import jax.numpy as jnp
import ml_dtypes
import numpy as np
from jax import lax
from jax.experimental import pallas as pl
from jax.experimental.pallas import tpu as pltpu
from jax.sharding import PartitionSpec as P

HEADS = 4
LEAF = 256
LEVELS = 5
HALF = LEAF // 2
BLOCKS = 4
EDGE_ROWS = 256
RIM_ROWS = 320
TABLE_ROWS = 896
L1_AT = 256
L2_AT = 640
FAR_ROWS = 192
HIDDEN = -1e30


def pooled(x, wide_ref):
    rows, width = x.shape
    parts = []
    for at in range(width // 128):
        wide_ref[at, 0:rows, :] = x[:, at * 128 : (at + 1) * 128].astype(jnp.float32)
        even = wide_ref[at, pl.ds(0, rows // 2, stride=2), :]
        odd = wide_ref[at, pl.ds(1, rows // 2, stride=2), :]
        parts.append(((even + odd) * 0.5).astype(x.dtype))
    return jnp.concatenate(parts, axis=1) if len(parts) > 1 else parts[0]


def pool_kernel(
    dev_ref, k_ref, v_ref, edge_ref, x1_ref, i1_ref, x2_ref, y_ref, l4_ref, l1_ref, wide_ref
):
    odd = dev_ref[0] % 2 == 1
    steps = pl.num_programs(0) // 2
    at = pl.program_id(0)

    def write(l0):
        l1 = pooled(l0[...], wide_ref)
        l2 = pooled(l1, wide_ref)
        l3 = pooled(l2, wide_ref)
        l4 = pooled(l3, wide_ref)
        l1_ref[...] = l1
        y_ref[0:128, :] = l3
        y_ref[128:192, :] = l4
        l4_ref[...] = l4
        i1_ref[L2_AT:TABLE_ROWS, :] = l2

        @pl.when(odd)
        def _():
            edge_ref[...] = l0[768:1024, :]
            x1_ref[0:128, :] = l1[256:384]
            x1_ref[128:256, :] = l2[0:128]
            x1_ref[256:320, :] = l2[0:64]
            i1_ref[0:256, :] = l0[0:256, :]
            i1_ref[L1_AT:L2_AT, :] = l1[0:384]
            x2_ref[0:128, :] = l2[0:128]
            x2_ref[128:192, :] = l3[64:128]

        @pl.when(jnp.logical_not(odd))
        def _():
            edge_ref[...] = l0[0:256, :]
            x1_ref[0:256, :] = l1[128:384]
            x1_ref[256:320, :] = l2[192:256]
            i1_ref[0:256, :] = l0[768:1024, :]
            i1_ref[L1_AT : L1_AT + 256, :] = l1[256:512]
            i1_ref[L1_AT + 256 : L2_AT, :] = l1[0:128]
            x2_ref[0:128, :] = l3
            x2_ref[128:192, :] = l3[64:128]

    @pl.when(at < steps)
    def _():
        write(k_ref)

    @pl.when(at >= steps)
    def _():
        write(v_ref)


def rim_kernel(relayed, dev_ref, edge_ref, via_ref, x1_ref, xt_ref, i2_ref, wide_ref):
    me = dev_ref[0]
    odd = me % 2 == 1
    if relayed:
        twice = functools.reduce(jnp.logical_or, [me == target for target in relayed])

        @pl.when(twice)
        def _():
            xt_ref[0:256, :] = via_ref[...]

        @pl.when(jnp.logical_not(twice))
        def _():
            xt_ref[0:256, :] = edge_ref[...]
    else:
        xt_ref[0:256, :] = edge_ref[...]

    @pl.when(odd)
    def _():
        l1 = jnp.concatenate([pooled(xt_ref[0:256, :], wide_ref), x1_ref[0:256, :]], axis=0)
        l2 = jnp.concatenate([pooled(l1, wide_ref), x1_ref[256:320, :]], axis=0)
        xt_ref[L1_AT:L2_AT, :] = l1
        xt_ref[L2_AT:TABLE_ROWS, :] = l2
        i2_ref[0:128, :] = l2[0:128]
        i2_ref[128:256, :] = pooled(l2, wide_ref)

    @pl.when(jnp.logical_not(odd))
    def _():
        l1 = jnp.concatenate([x1_ref[0:128, :], pooled(xt_ref[0:256, :], wide_ref)], axis=0)
        l2 = jnp.concatenate([x1_ref[128:256, :], pooled(l1, wide_ref)], axis=0)
        xt_ref[L1_AT : L1_AT + 256, :] = l1
        xt_ref[L1_AT + 256 : L2_AT, :] = l1[0:128]
        xt_ref[L2_AT:TABLE_ROWS, :] = l2
        l3 = pooled(l2, wide_ref)
        i2_ref[0:128, :] = l3
        i2_ref[128:256, :] = l3


def offset_lanes(level, valid, scale):
    terms = []
    rest = level / scale
    for _ in range(3):
        term = float(np.float32(rest).astype(ml_dtypes.bfloat16))
        terms.append(term)
        rest -= term
    if valid is not None:
        terms = [jnp.where(valid, t, h) for t, h in zip(terms, (HIDDEN, 0.0, 0.0))]
    lane = lax.broadcasted_iota(jnp.int32, (128, 128), 1)
    lanes = jnp.zeros((128, 128), jnp.float32)
    for at, term in enumerate(terms):
        lanes = jnp.where(lane == at, term, lanes)
    return lanes.astype(jnp.bfloat16)


def chunks_of(segments):
    chunks = [[]]
    room = 256
    for k_ref, v_ref, start, count, lanes in segments:
        while count:
            take = min(count, room, 128)
            chunks[-1].append((k_ref, v_ref, start, take, lanes))
            start, count, room = start + take, count - take, room - take
            if not room:
                chunks.append([])
                room = 256
    return [chunk for chunk in chunks if chunk]


def attend(query, segments, scale, before):
    rows = query.shape[0]
    lane = lax.broadcasted_iota(jnp.int32, query.shape, 1)
    query = jnp.concatenate([query, jnp.where(lane < 3, 1.0, 0.0).astype(query.dtype)], axis=1)
    chunks = chunks_of(segments)
    scores = []
    peak = None
    for chunk in chunks:
        keys = jnp.concatenate(
            [
                jnp.concatenate([k_ref[start : start + count, :], lanes[0:count]], axis=1)
                for k_ref, _, start, count, lanes in chunk
            ],
            axis=0,
        )
        score = lax.dot_general(
            query, keys, (((1,), (1,)), ((), ())), preferred_element_type=jnp.float32
        )
        scores.append(score)
        for col in range(0, keys.shape[0], 128):
            top = score[:, col : col + 128]
            peak = top if peak is None else jnp.maximum(peak, top)
    peak = jnp.max(peak, axis=1, keepdims=True) * scale
    if before is not None:
        peak = jnp.maximum(peak, before)
    out = None
    for chunk, score in zip(chunks, scores):
        weight = jnp.exp2(score * scale - peak).astype(jnp.bfloat16)
        values = jnp.concatenate(
            [v_ref[start : start + count, :] for _, v_ref, start, count, _ in chunk], axis=0
        )
        table = jnp.concatenate([values, jnp.ones((values.shape[0], 128), jnp.bfloat16)], axis=1)
        part = jnp.dot(weight, table, preferred_element_type=jnp.float32)
        out = part if out is None else out + part
    return peak, out[:, 0:128], out[:, 128:256]


def base_two_scale(head_size):
    return math.log2(math.e) / math.sqrt(head_size)


def near_kernel(dev_ref, q_ref, k_ref, v_ref, l1k, l1v, mk, mv, *sums):
    scale = base_two_scale(q_ref.shape[1])
    zero = offset_lanes(0, None, scale)
    one = offset_lanes(1, None, scale)
    two = offset_lanes(2, None, scale)
    own = ((256, 256), None, (0, 128), (0, 256))

    def run(odd):
        if odd:
            mate = (
                [(mk, mv, 0, 256, zero), (mk, mv, L1_AT, 128, one), (mk, mv, L2_AT, 128, two)],
                [(mk, mv, L1_AT, 256, one), (mk, mv, L2_AT, 128, two)],
                [(mk, mv, L2_AT, 256, two)],
                [(mk, mv, L2_AT, 256, two)],
            )
        else:
            mate = (
                [(mk, mv, L2_AT, 256, two)],
                [(mk, mv, L1_AT, 128, one), (mk, mv, L2_AT, 256, two)],
                [(mk, mv, L1_AT, 256, one)],
                [(mk, mv, 0, 256, zero), (mk, mv, L1_AT + 256, 128, one)],
            )
        for block in range(BLOCKS):
            low, high = max(block - 1, 0), min(block + 2, BLOCKS)
            segments = [(k_ref, v_ref, low * LEAF, (high - low) * LEAF, zero)]
            if own[block]:
                segments.append((l1k, l1v, own[block][0], own[block][1], one))
            here = slice(block * LEAF, (block + 1) * LEAF)
            peak, acc, total = attend(q_ref[here, :], segments + mate[block], scale, None)
            write_sums(sums, here, peak, acc, total)

    @pl.when(dev_ref[0] % 2 == 1)
    def _():
        run(True)

    @pl.when(dev_ref[0] % 2 == 0)
    def _():
        run(False)


def read_mass(mass_ref, here):
    packed = mass_ref[here, :]
    lane = lax.broadcasted_iota(jnp.int32, packed.shape, 1)
    own = jnp.where(lane == pl.program_id(0), packed, 0.0)
    return jnp.sum(own, axis=1, keepdims=True)


def write_sums(sums, here, peak, acc, total):
    mean_ref, mass_ref = sums
    mean_ref[here, :] = acc / total
    lane = lax.broadcasted_iota(jnp.int32, acc.shape, 1)
    mass = peak + jnp.log2(total)
    kept = jnp.where(pl.program_id(0) == 0, 0.0, mass_ref[here, :])
    mass_ref[here, :] = jnp.where(lane == pl.program_id(0), mass, kept)


def attend_after(query, segments, scale, stats, here):
    mean_ref, mass_ref = stats
    mass = read_mass(mass_ref, here)
    peak, acc, total = attend(query, segments, scale, mass)
    factor = jnp.exp2(mass - peak)
    return peak, mean_ref[here, :] * factor + acc, total + factor


def far_kernel(flow_spans, count, dev_ref, q_ref, *refs):
    xk, xv, i2k, i2v, x2k, x2v, x2mk, x2mv = refs[0:8]
    stats, out_ref, wide_ref = refs[-4:-2], refs[-2], refs[-1]
    flow_refs = [refs[8 + 4 * at : 12 + 4 * at] for at in range(len(flow_spans))]
    scale = base_two_scale(q_ref.shape[1])
    me = dev_ref[0]
    chip = me // 2
    chips = count // 2

    def lanes(level, valid):
        return offset_lanes(level, valid, scale)

    quads = []
    for shifts, (yk, yv, ymk, ymv) in zip(flow_spans, flow_refs):
        valid = False
        for shift in shifts:
            source = chip - shift // 2
            here = (source >= 0) & (source < chips)
            if shift == -4:
                here = here & (chip % 2 == 0)
            if shift == 6:
                here = here & (chip % 2 == 1)
            valid = here | valid
        four = lanes(4, valid)
        start = yk.shape[0] - 64
        quads += [(yk, yv, start, 64, four), (ymk, ymv, start, 64, four)]

    def run(odd):
        near = (me < count - 1) if odd else (me >= 1)
        zero, one, two = (lanes(level, near) for level in range(3))
        beyond = lanes(2, me + 2 < count)
        if odd:
            ymk, ymv = flow_refs[0][2:4]
            coarse = [
                (ymk, ymv, 0, 128, lanes(3, me + 3 < count)),
                (x2k, x2v, 0, 128, lanes(3, me - 3 >= 0)),
                (i2k, i2v, 0, 128, lanes(3, me - 2 >= 0)),
            ]
            skip = (x2mk, x2mv, 0, 128, beyond)
            rim = (
                [(xk, xv, L2_AT, 256, two)],
                [(xk, xv, L2_AT, 256, two), (xk, xv, L1_AT, 128, one)],
                [(xk, xv, L1_AT, 256, one), skip],
                [(xk, xv, 0, 256, zero), (xk, xv, L1_AT + 256, 128, one), skip],
            )
        else:
            third = [
                jnp.concatenate([pooled(table[0:128, :], wide_ref), table[128:192, :]], axis=0)
                for table in (x2k, x2v)
            ]
            coarse = [
                (x2mk, x2mv, 0, 128, lanes(3, me - 2 >= 0)),
                (third[0], third[1], 0, 128, lanes(3, me + 3 < count)),
                (i2k, i2v, 128, 128, lanes(3, me + 2 < count)),
            ]
            skip = (i2k, i2v, 0, 128, beyond)
            rim = (
                [(xk, xv, 0, 256, zero), (xk, xv, L1_AT, 128, one), (xk, xv, L2_AT, 128, two)],
                [(xk, xv, L1_AT, 256, one), (xk, xv, L2_AT, 128, two)],
                [(xk, xv, L2_AT, 256, two), skip],
                [(xk, xv, L2_AT, 256, two), skip],
            )
        for block in range(BLOCKS):
            here = slice(block * LEAF, (block + 1) * LEAF)
            segments = quads + coarse[0:2] + rim[block] + coarse[2:3]
            _, acc, total = attend_after(q_ref[here, :], segments, scale, stats, here)
            out_ref[here, :] = (acc / total).astype(out_ref.dtype)

    @pl.when(me % 2 == 1)
    def _():
        run(True)

    @pl.when(me % 2 == 0)
    def _():
        run(False)


def relays(count):
    return {(3, 4): 7, (4, 3): 0} if count == 8 else {}


def flow_pairs(shifts, count):
    pairs = []
    for shift in shifts:
        for source in range(count):
            target = source + shift
            if 0 <= target < count and not (shift == 6 and target // 2 % 2 == 0):
                pairs.append((source, target))
    return pairs


def far_flows(count):
    spans = []
    for low, high in ((-4, 4), (-6, 6)):
        pairs = flow_pairs((low, high), count)
        unique = len({s for s, _ in pairs}) == len(pairs) == len({t for _, t in pairs})
        spans.extend([(low, high)] if unique else [(low,), (high,)])
    return tuple(spans)


def on_device(query_rows, key_rows, value_rows):
    token_rows, width = query_rows.shape
    head_size = width // HEADS
    count = lax.axis_size("ctx")
    me = lax.axis_index("ctx").astype(jnp.int32).reshape(1)
    dtype = key_rows.dtype

    def shape(rows, columns=2 * width, kind=dtype):
        return jax.ShapeDtypeStruct((rows, columns), kind)

    smem = pl.BlockSpec(memory_space=pltpu.SMEM)
    params = pltpu.CompilerParams(vmem_limit_bytes=64 << 20)

    near = range(1, count - 1, 2)
    across = [(i, i + 1) for i in near] + [(i + 1, i) for i in near]
    detours = relays(count)
    cut = width

    def column(rows):
        return pl.BlockSpec((rows, cut), lambda j: (0, j))

    pooled_rows = (EDGE_ROWS, RIM_ROWS, TABLE_ROWS, FAR_ROWS, 192, 64, token_rows // 2)
    edge, x1s, i1s, x2s, ys, l4, l1 = pl.pallas_call(
        pool_kernel,
        name="pool",
        grid=(2,),
        out_shape=[shape(rows) for rows in pooled_rows],
        in_specs=[
            smem,
            pl.BlockSpec((token_rows, cut), lambda j: (0, 0)),
            pl.BlockSpec((token_rows, cut), lambda j: (0, 0)),
        ],
        out_specs=[column(rows) for rows in pooled_rows],
        scratch_shapes=[pltpu.VMEM((cut // 128, token_rows, 128), jnp.float32)],
        compiler_params=params,
        cost_estimate=pl.CostEstimate(flops=0, transcendentals=0, bytes_accessed=24 << 20),
    )(me, key_rows, value_rows)

    edge_r = lax.ppermute(edge, "ctx", [(s, detours.get((s, t), t)) for s, t in across])
    x2r = lax.ppermute(
        x2s,
        "ctx",
        [(i, i + 3) for i in range(0, count - 3, 2)] + [(i, i - 3) for i in range(3, count, 2)],
    )
    flow_spans = far_flows(count)
    yrs = [
        lax.ppermute(ys if abs(shifts[0]) == 4 else l4, "ctx", flow_pairs(shifts, count))
        for shifts in flow_spans
    ]
    x1r = lax.ppermute(x1s, "ctx", across)
    mates = [(i, i ^ 1) for i in range(count)]
    i1r = lax.ppermute(i1s, "ctx", mates)
    edge_r, i1r = lax.optimization_barrier((edge_r, i1r))
    via_r = edge_r
    if detours:
        via_r = lax.ppermute(edge_r, "ctx", [(via, t) for (_, t), via in detours.items()])

    def head(rows, base=0):
        return pl.BlockSpec((rows, head_size), lambda h, *_: (0, base + h))

    def attention(kernel, name, keys, tables, stats, last=False):
        arrays, specs = [], []
        for table in tables:
            if isinstance(table, tuple):
                arrays += table
                specs += [head(table[0].shape[0])] * 2
            else:
                arrays += [table, table]
                specs += [head(table.shape[0]), head(table.shape[0], HEADS)]
        pairs = token_rows * keys * HEADS
        sums = [shape(token_rows, width, jnp.float32), shape(token_rows, 128, jnp.float32)]
        sum_specs = [head(token_rows), pl.BlockSpec((token_rows, 128), lambda h: (0, 0))]
        return pl.pallas_call(
            kernel,
            name=name,
            grid=(HEADS,),
            out_shape=shape(token_rows, width) if last else sums,
            in_specs=[smem, head(token_rows)] + specs + (sum_specs if stats else []),
            out_specs=head(token_rows) if last else sum_specs,
            scratch_shapes=[pltpu.VMEM((head_size // 128, 128, 128), jnp.float32)] if last else [],
            compiler_params=params,
            cost_estimate=pl.CostEstimate(
                flops=4 * pairs * head_size, transcendentals=pairs, bytes_accessed=12 << 20
            ),
        )(me, query_rows, *arrays, *stats)

    stats = attention(
        near_kernel,
        "near",
        1152,
        [(key_rows, value_rows), l1, i1r],
        (),
    )
    x2r, yrs, stats = lax.optimization_barrier((x2r, yrs, stats))
    tables = [x2r, lax.ppermute(x2r, "ctx", mates)]
    for yr in yrs:
        tables += [yr, lax.ppermute(yr, "ctx", mates)]
    edge_r, via_r, x1r, stats = lax.optimization_barrier((edge_r, via_r, x1r, stats))
    xt, i2s = pl.pallas_call(
        functools.partial(rim_kernel, [t for _, t in detours]),
        name="rim",
        grid=(2,),
        out_shape=[shape(TABLE_ROWS), shape(256)],
        in_specs=[smem, column(EDGE_ROWS), column(EDGE_ROWS), column(RIM_ROWS)],
        out_specs=[column(TABLE_ROWS), column(256)],
        scratch_shapes=[pltpu.VMEM((cut // 128, 384, 128), jnp.float32)],
        compiler_params=params,
    )(me, edge_r, via_r, x1r)
    i2r = lax.ppermute(i2s, "ctx", mates)
    kernel = functools.partial(far_kernel, flow_spans, count)
    return attention(kernel, "far", 1088, [xt, i2r] + tables, stats, True)


def solution(mesh):
    spec = P(("dp", "ctx"), None)
    return jax.shard_map(
        on_device, mesh=mesh, in_specs=(spec, spec, spec), out_specs=spec, check_vma=False
    )
```

time: 65.8 us -> 57.1 us (0.87)
  the two profiles are of different devices: /device:TPU:0 before, /device:TPU:27 now
where the time goes in v2:
time: 57.1 us; the launch traced here: 56.8 us
  Pallas kernels  28.1 us (49%)
  starting transfers between devices  15.9 us (28%)
  waiting for transfers between devices  12.8 us (22%)
    pallas_call x2, Pallas kernels, attention(): pl.pallas_call(kernel, name=name, grid=(HEADS,), out_shape=shape(token_ro...  20.7 us
    ppermute x1, starting transfers between devices, on_device(): lax.ppermute(x2s, 'ctx', [(i, i + 3) for i in range(0, count - 3, 2)] + [...  5.06 us
    pallas_call x1, Pallas kernels, on_device(): pl.pallas_call(pool_kernel, name='pool', grid=(2,), out_shape=[shape(rows...  4.56 us
    ppermute x2, waiting for transfers between devices, on_device(): lax.ppermute(ys if abs(shifts[0]) == 4 else l4, 'ctx', flow_pairs(shifts,...  4.49 us
    ppermute x1, starting transfers between devices, on_device(): lax.ppermute(edge, 'ctx', [(s, detours.get((s, t), t)) for s, t in across])  3.94 us
    ppermute x1, waiting for transfers between devices, on_device(): lax.ppermute(edge, 'ctx', [(s, detours.get((s, t), t)) for s, t in across])  3.35 us
    pallas_call x1, Pallas kernels, on_device(): pl.pallas_call(functools.partial(rim_kernel, [t for _, t in detours]), na...  2.86 us
    ppermute x2, waiting for transfers between devices, on_device(): tables += [yr, lax.ppermute(yr, 'ctx', mates)]  2.63 us
  transfers between devices with their start and end apart: 11, of which 4 were waited for; matrix products, arithmetic and copies ran while one was open for 0% of the time, Pallas kernels for 17%

profile of v2, /device:TPU:27, one launch (start us, length us, event | category | flops | bytes accessed | tf_op | source)
XLA Modules:
  0.0 56.8 jit_solution(5484201455837784690)
XLA Ops:
  0.0 4.6 %pool.1 = (bf16[256,1024]{1,0:T(8,128)(2,1)}, bf16[320,1024]{1,0:T(8,128)(2,1)}, bf16[896,1024]{1,0:T(8,128)(2,1)}, bf16[192,1024]{1,0:T(8,128)(2,1)}, bf16[192,...) custom-call(s32[1]{0:T(128)} %bitcast.dev_ref, bf16[1024,512]{1,0:T(8,128)(2,1)} %k_ref.3, ...), custom_call_target="tpu_custom_call" | custom-call | bytes 25165824 | tf_op jit(solution)/shard_map/pool/pallas_call | solution.py:381
  4.6 0.7 %collective-permute-start.1 = (bf16[896,1024]{1,0:T(8,128)(2,1)}, bf16[896,1024]{1,0:T(8,128)(2,1)}, u32[]{:S(2)}, u32[]{:S(2)}) collective-permute-start(bf16[896,1024]{1,0:T(8,128)(2,1)} %get-tuple-element.29), channel_id=1, source_target_pairs={{0,4},{4,0},{8,12},{12,8},{16,20},{20,16},{24,28},{28,24},{1,5},{5... | collective-permute-start | bytes 5505032 | tf_op jit(solution)/shard_map/ppermute | solution.py:410
  5.2 3.9 %collective-permute-start = (bf16[256,1024]{1,0:T(8,128)(2,1)}, bf16[256,1024]{1,0:T(8,128)(2,1)}, u32[]{:S(2)}, u32[]{:S(2)}) collective-permute-start(bf16[256,1024]{1,0:T(8,128)(2,1)} %get-tuple-element.28), channel_id=1, source_target_pairs={{4,8},{12,28},{20,24},{8,4},{16,0},{24,20},{5,9},{13,29},{21,25},{... | collective-permute-start | bytes 1572872 | tf_op jit(solution)/shard_map/ppermute | solution.py:397
  9.2 2.3 %collective-permute-start.3 = (bf16[320,1024]{1,0:T(8,128)(2,1)}, bf16[320,1024]{1,0:T(8,128)(2,1)}, u32[]{:S(2)}, u32[]{:S(2)}) collective-permute-start(bf16[320,1024]{1,0:T(8,128)(2,1)} %get-tuple-element.31), channel_id=1, source_target_pairs={{4,8},{12,16},{20,24},{8,4},{16,12},{24,20},{5,9},{13,17},{21,25},... | collective-permute-start | bytes 1966088 | tf_op jit(solution)/shard_map/ppermute | solution.py:408
  11.5 3.3 %collective-permute-done.edge_ref = bf16[256,1024]{1,0:T(8,128)(2,1)} collective-permute-done((bf16[256,1024]{1,0:T(8,128)(2,1)}, bf16[256,1024]{1,0:T(8,128)(2,1)}, u32[]{:S(2)}, u32[]{:S(2)}) %collective-permute-start) | collective-permute-done | bytes 524320 | tf_op jit(solution)/shard_map/ppermute | solution.py:397
  14.8 0.0 collective-permute-done.1.mk.mv
  14.8 1.3 %collective-permute-start.2 = (bf16[256,1024]{1,0:T(8,128)(2,1)}, bf16[256,1024]{1,0:T(8,128)(2,1)}, u32[]{:S(2)}, u32[]{:S(2)}) collective-permute-start(bf16[256,1024]{1,0:T(8,128)(2,1)} %collective-permute-done.edge_ref), channel_id=1, source_target_pairs={{28,16},{0,12},{29,17},{1,13},{30,18},{2,14},{31,19},{3,15}} | collective-permute-start | bytes 1572872 | tf_op jit(solution)/shard_map/ppermute | solution.py:414
  16.1 5.1 %collective-permute-start.4 = (bf16[192,1024]{1,0:T(8,128)(2,1)}, bf16[192,1024]{1,0:T(8,128)(2,1)}, u32[]{:S(2)}, u32[]{:S(2)}) collective-permute-start(bf16[192,1024]{1,0:T(8,128)(2,1)} %get-tuple-element.32), channel_id=1, source_target_pairs={{0,12},{8,20},{16,28},{12,0},{20,8},{28,16},{1,13},{9,21},{17,29},... | collective-permute-start | bytes 1179656 | tf_op jit(solution)/shard_map/ppermute | solution.py:398
  21.2 0.1 collective-permute-start.5
  21.2 1.3 %collective-permute-start.6 = (bf16[64,1024]{1,0:T(8,128)(2,1)}, bf16[64,1024]{1,0:T(8,128)(2,1)}, u32[]{:S(2)}, u32[]{:S(2)}) collective-permute-start(bf16[64,1024]{1,0:T(8,128)(2,1)} %get-tuple-element.34), channel_id=1, source_target_pairs={{24,0},{28,4},{0,24},{4,28},{25,1},{29,5},{1,25},{5,29},{26,2},{30... | collective-permute-start | bytes 393224 | tf_op jit(solution)/shard_map/ppermute | solution.py:405
  22.6 9.9 %near.1 = (f32[1024,512]{1,0:T(8,128)}, f32[1024,128]{1,0:T(8,128)}) custom-call(s32[1]{0:T(128)} %bitcast.dev_ref, bf16[1024,512]{1,0:T(8,128)(2,1)} %q_ref.3, bf16[1024,512]{1,0:T(8,128)(2,1)} %k_ref.3, bf16[1024,512]{1,0:T(8,128)(2,1)} %v_ref.3, bf16[512,1024]{1,0:T(8,128)(2,1)} %get-tuple-element.35.l1k.l1v, ...), custom_call_target="tpu_custom_call" | custom-call | flops 2415919104 | bytes 12582912 | tf_op jit(solution)/shard_map/near/pallas_call | solution.py:431
  32.5 0.0 collective-permute-done.6.refs_12_.refs_13_
  32.5 2.3 %collective-permute-done.4.refs_4_.refs_5_ = bf16[192,1024]{1,0:T(8,128)(2,1)} collective-permute-done((bf16[192,1024]{1,0:T(8,128)(2,1)}, bf16[192,1024]{1,0:T(8,128)(2,1)}, u32[]{:S(2)}, u32[]{:S(2)}) %collective-permute-start.4) | collective-permute-done | bytes 393248 | tf_op jit(solution)/shard_map/ppermute | solution.py:398
  34.8 4.5 %collective-permute-done.5.refs_8_.refs_9_ = bf16[192,1024]{1,0:T(8,128)(2,1)} collective-permute-done((bf16[192,1024]{1,0:T(8,128)(2,1)}, bf16[192,1024]{1,0:T(8,128)(2,1)}, u32[]{:S(2)}, u32[]{:S(2)}) %collective-permute-start.5) | collective-permute-done | bytes 393248 | tf_op jit(solution)/shard_map/ppermute | solution.py:405
  39.3 0.0 collective-permute-done.2.via_ref
  39.3 2.9 %rim.1 = (bf16[896,1024]{1,0:T(8,128)(2,1)}, bf16[256,1024]{1,0:T(8,128)(2,1)}) custom-call(s32[1]{0:T(128)} %bitcast.dev_ref, bf16[256,1024]{1,0:T(8,128)(2,1)} %collective-permute-done.edge_ref, bf16[256,1024]{1,0:T(8,128)(2,1)} %collective-permute-done.2.via_ref, bf16[320,1024]{1,0:T(8,128)(2,1)} %collective-permute-done.3.x1_ref), custom_call_target="tpu_custom_call" | custom-call | tf_op jit(solution)/shard_map/rim/pallas_call | solution.py:457
  42.1 0.7 %collective-permute-start.7 = (bf16[256,1024]{1,0:T(8,128)(2,1)}, bf16[256,1024]{1,0:T(8,128)(2,1)}, u32[]{:S(2)}, u32[]{:S(2)}) collective-permute-start(bf16[256,1024]{1,0:T(8,128)(2,1)} %get-tuple-element.45), channel_id=1, source_target_pairs={{0,4},{4,0},{8,12},{12,8},{16,20},{20,16},{24,28},{28,24},{1,5},{5... | collective-permute-start | bytes 1572872 | tf_op jit(solution)/shard_map/ppermute | solution.py:467
  42.8 0.1 collective-permute-start.8
  42.9 0.5 collective-permute-start.9
  43.3 0.1 collective-permute-start.10
  43.4 2.6 %collective-permute-done.10.refs_14_.refs_15_ = bf16[64,1024]{1,0:T(8,128)(2,1)} collective-permute-done((bf16[64,1024]{1,0:T(8,128)(2,1)}, bf16[64,1024]{1,0:T(8,128)(2,1)}, u32[]{:S(2)}, u32[]{:S(2)}) %collective-permute-start.10) | collective-permute-done | bytes 131104 | tf_op jit(solution)/shard_map/ppermute | solution.py:455
  46.0 0.0 collective-permute-done.9.refs_10_.refs_11_
  46.0 0.0 collective-permute-done.7.refs_2_.refs_3_
  46.0 10.8 %far.1 = bf16[1024,512]{1,0:T(8,128)(2,1)} custom-call(s32[1]{0:T(128)} %bitcast.dev_ref, bf16[1024,512]{1,0:T(8,128)(2,1)} %q_ref.3, bf16[896,1024]{1,0:T(8,128)(2,1)} %get-tuple-element.44.refs_0_.refs_1_, bf16[896,1024]{1,0:T(8,128)(2,1)} %get-tuple-element.44.refs_0_.refs_1_, bf16[256,1024]{1,0:T(8,128)(2,1)} %collective-permute-done.7.refs_2_.refs_3_, ...), custom_call_target="tpu_custom_call" | custom-call | flops 2281701376 | bytes 12582912 | tf_op jit(solution)/shard_map/far/pallas_call | solution.py:431
  (2 shorter events, 0.0 us)
Async XLA Ops:
  4.6 10.2 %collective-permute-start.1 = (bf16[896,1024]{1,0:T(8,128)(2,1)}, bf16[896,1024]{1,0:T(8,128)(2,1)}, u32[]{:S(2)}, u32[]{:S(2)}) collective-permute-start(bf16[896,1024]{1,0:T(8,128)(2,1)} %get-tuple-element.29), channel_id=1, source_target_pairs={{0,4},{4,0},{8,12},{12,8},{16,20},{20,16},{24,28},{28,24},{1,5},{5... | collective-permute-start | bytes 5505032 | tf_op jit(solution)/shard_map/ppermute | solution.py:410
  5.2 9.6 %collective-permute-start = (bf16[256,1024]{1,0:T(8,128)(2,1)}, bf16[256,1024]{1,0:T(8,128)(2,1)}, u32[]{:S(2)}, u32[]{:S(2)}) collective-permute-start(bf16[256,1024]{1,0:T(8,128)(2,1)} %get-tuple-element.28), channel_id=1, source_target_pairs={{4,8},{12,28},{20,24},{8,4},{16,0},{24,20},{5,9},{13,29},{21,25},{... | collective-permute-start | bytes 1572872 | tf_op jit(solution)/shard_map/ppermute | solution.py:397
  9.2 30.1 %collective-permute-start.3 = (bf16[320,1024]{1,0:T(8,128)(2,1)}, bf16[320,1024]{1,0:T(8,128)(2,1)}, u32[]{:S(2)}, u32[]{:S(2)}) collective-permute-start(bf16[320,1024]{1,0:T(8,128)(2,1)} %get-tuple-element.31), channel_id=1, source_target_pairs={{4,8},{12,16},{20,24},{8,4},{16,12},{24,20},{5,9},{13,17},{21,25},... | collective-permute-start | bytes 1966088 | tf_op jit(solution)/shard_map/ppermute | solution.py:408
  14.8 24.5 %collective-permute-start.2 = (bf16[256,1024]{1,0:T(8,128)(2,1)}, bf16[256,1024]{1,0:T(8,128)(2,1)}, u32[]{:S(2)}, u32[]{:S(2)}) collective-permute-start(bf16[256,1024]{1,0:T(8,128)(2,1)} %collective-permute-done.edge_ref), channel_id=1, source_target_pairs={{28,16},{0,12},{29,17},{1,13},{30,18},{2,14},{31,19},{3,15}} | collective-permute-start | bytes 1572872 | tf_op jit(solution)/shard_map/ppermute | solution.py:414
  16.1 18.7 %collective-permute-start.4 = (bf16[192,1024]{1,0:T(8,128)(2,1)}, bf16[192,1024]{1,0:T(8,128)(2,1)}, u32[]{:S(2)}, u32[]{:S(2)}) collective-permute-start(bf16[192,1024]{1,0:T(8,128)(2,1)} %get-tuple-element.32), channel_id=1, source_target_pairs={{0,12},{8,20},{16,28},{12,0},{20,8},{28,16},{1,13},{9,21},{17,29},... | collective-permute-start | bytes 1179656 | tf_op jit(solution)/shard_map/ppermute | solution.py:398
  21.2 18.1 %collective-permute-start.5 = (bf16[192,1024]{1,0:T(8,128)(2,1)}, bf16[192,1024]{1,0:T(8,128)(2,1)}, u32[]{:S(2)}, u32[]{:S(2)}) collective-permute-start(bf16[192,1024]{1,0:T(8,128)(2,1)} %get-tuple-element.33), channel_id=1, source_target_pairs={{16,0},{20,4},{24,8},{28,12},{0,16},{4,20},{8,24},{12,28},{17,1},{... | collective-permute-start | bytes 1179656 | tf_op jit(solution)/shard_map/ppermute | solution.py:405
  21.2 11.2 %collective-permute-start.6 = (bf16[64,1024]{1,0:T(8,128)(2,1)}, bf16[64,1024]{1,0:T(8,128)(2,1)}, u32[]{:S(2)}, u32[]{:S(2)}) collective-permute-start(bf16[64,1024]{1,0:T(8,128)(2,1)} %get-tuple-element.34), channel_id=1, source_target_pairs={{24,0},{28,4},{0,24},{4,28},{25,1},{29,5},{1,25},{5,29},{26,2},{30... | collective-permute-start | bytes 393224 | tf_op jit(solution)/shard_map/ppermute | solution.py:405
  42.1 3.9 %collective-permute-start.7 = (bf16[256,1024]{1,0:T(8,128)(2,1)}, bf16[256,1024]{1,0:T(8,128)(2,1)}, u32[]{:S(2)}, u32[]{:S(2)}) collective-permute-start(bf16[256,1024]{1,0:T(8,128)(2,1)} %get-tuple-element.45), channel_id=1, source_target_pairs={{0,4},{4,0},{8,12},{12,8},{16,20},{20,16},{24,28},{28,24},{1,5},{5... | collective-permute-start | bytes 1572872 | tf_op jit(solution)/shard_map/ppermute | solution.py:467
  42.8 3.2 %collective-permute-start.8 = (bf16[192,1024]{1,0:T(8,128)(2,1)}, bf16[192,1024]{1,0:T(8,128)(2,1)}, u32[]{:S(2)}, u32[]{:S(2)}) collective-permute-start(bf16[192,1024]{1,0:T(8,128)(2,1)} %collective-permute-done.4.refs_4_.refs_5_), channel_id=1, source_target_pairs={{0,4},{4,0},{8,12},{12,8},{16,20},{20,16},{24,28},{28,24},{1,5},{5... | collective-permute-start | bytes 1179656 | tf_op jit(solution)/shard_map/ppermute | solution.py:453
  42.9 3.1 %collective-permute-start.9 = (bf16[192,1024]{1,0:T(8,128)(2,1)}, bf16[192,1024]{1,0:T(8,128)(2,1)}, u32[]{:S(2)}, u32[]{:S(2)}) collective-permute-start(bf16[192,1024]{1,0:T(8,128)(2,1)} %collective-permute-done.5.refs_8_.refs_9_), channel_id=1, source_target_pairs={{0,4},{4,0},{8,12},{12,8},{16,20},{20,16},{24,28},{28,24},{1,5},{5... | collective-permute-start | bytes 1179656 | tf_op jit(solution)/shard_map/ppermute | solution.py:455
  43.3 2.7 %collective-permute-start.10 = (bf16[64,1024]{1,0:T(8,128)(2,1)}, bf16[64,1024]{1,0:T(8,128)(2,1)}, u32[]{:S(2)}, u32[]{:S(2)}) collective-permute-start(bf16[64,1024]{1,0:T(8,128)(2,1)} %collective-permute-done.6.refs_12_.refs_13_), channel_id=1, source_target_pairs={{0,4},{4,0},{8,12},{12,8},{16,20},{20,16},{24,28},{28,24},{1,5},{5... | collective-permute-start | bytes 393224 | tf_op jit(solution)/shard_map/ppermute | solution.py:455

commit v3 on v2

--- a/solution.py
+++ b/solution.py
@@ -22,6 +22,7 @@
 L2_AT = 640
 FAR_ROWS = 192
 HIDDEN = -1e30
+SAFE_TOTAL = 2.0**100
 
 
 def pooled(x, wide_ref):
@@ -151,7 +152,7 @@
     return [chunk for chunk in chunks if chunk]
 
 
-def attend(query, segments, scale, before):
+def attend(query, segments, scale, before, exact):
     rows = query.shape[0]
     lane = lax.broadcasted_iota(jnp.int32, query.shape, 1)
     query = jnp.concatenate([query, jnp.where(lane < 3, 1.0, 0.0).astype(query.dtype)], axis=1)
@@ -170,12 +171,17 @@
             query, keys, (((1,), (1,)), ((), ())), preferred_element_type=jnp.float32
         )
         scores.append(score)
+        if not exact and (peak is not None or before is not None):
+            continue
         for col in range(0, keys.shape[0], 128):
             top = score[:, col : col + 128]
             peak = top if peak is None else jnp.maximum(peak, top)
-    peak = jnp.max(peak, axis=1, keepdims=True) * scale
-    if before is not None:
-        peak = jnp.maximum(peak, before)
+    if peak is None:
+        peak = before
+    else:
+        peak = jnp.max(peak, axis=1, keepdims=True) * scale
+        if before is not None:
+            peak = jnp.maximum(peak, before)
     out = None
     for chunk, score in zip(chunks, scores):
         weight = jnp.exp2(score * scale - peak).astype(jnp.bfloat16)
@@ -214,14 +220,17 @@
                 [(mk, mv, L1_AT, 256, one)],
                 [(mk, mv, 0, 256, zero), (mk, mv, L1_AT + 256, 128, one)],
             )
-        for block in range(BLOCKS):
+        def one_block(block, exact):
             low, high = max(block - 1, 0), min(block + 2, BLOCKS)
             segments = [(k_ref, v_ref, low * LEAF, (high - low) * LEAF, zero)]
             if own[block]:
                 segments.append((l1k, l1v, own[block][0], own[block][1], one))
             here = slice(block * LEAF, (block + 1) * LEAF)
-            peak, acc, total = attend(q_ref[here, :], segments + mate[block], scale, None)
+            peak, acc, total = attend(q_ref[here, :], segments + mate[block], scale, None, exact)
             write_sums(sums, here, peak, acc, total)
+            return total
+
+        all_blocks(one_block)
 
     @pl.when(dev_ref[0] % 2 == 1)
     def _():
@@ -248,10 +257,24 @@
     mass_ref[here, :] = jnp.where(lane == pl.program_id(0), mass, kept)
 
 
-def attend_after(query, segments, scale, stats, here):
+def all_blocks(one_block):
+    largest = None
+    for block in range(BLOCKS):
+        total = one_block(block, False)
+        largest = total if largest is None else jnp.maximum(largest, total)
+
+    @pl.when(jnp.logical_not(jnp.max(largest) < SAFE_TOTAL))
+    def _():
+        for block in range(BLOCKS):
+            one_block(block, True)
+
+
+def attend_after(query, segments, scale, stats, here, exact):
     mean_ref, mass_ref = stats
     mass = read_mass(mass_ref, here)
-    peak, acc, total = attend(query, segments, scale, mass)
+    peak, acc, total = attend(query, segments, scale, mass, exact)
+    if not exact:
+        return peak, mean_ref[here, :] + acc, total + 1.0
     factor = jnp.exp2(mass - peak)
     return peak, mean_ref[here, :] * factor + acc, total + factor
 
@@ -318,11 +341,14 @@
                 [(xk, xv, L2_AT, 256, two), skip],
                 [(xk, xv, L2_AT, 256, two), skip],
             )
-        for block in range(BLOCKS):
+        def one_block(block, exact):
             here = slice(block * LEAF, (block + 1) * LEAF)
             segments = quads + coarse[0:2] + rim[block] + coarse[2:3]
-            _, acc, total = attend_after(q_ref[here, :], segments, scale, stats, here)
+            _, acc, total = attend_after(q_ref[here, :], segments, scale, stats, here, exact)
             out_ref[here, :] = (acc / total).astype(out_ref.dtype)
+            return total
+
+        all_blocks(one_block)
 
     @pl.when(me % 2 == 1)
     def _():
@@ -401,17 +427,11 @@
         [(i, i + 3) for i in range(0, count - 3, 2)] + [(i, i - 3) for i in range(3, count, 2)],
     )
     flow_spans = far_flows(count)
-    yrs = [
-        lax.ppermute(ys if abs(shifts[0]) == 4 else l4, "ctx", flow_pairs(shifts, count))
-        for shifts in flow_spans
-    ]
+    steps = [shifts for shifts in flow_spans if abs(shifts[0]) == 4]
+    yrs = [lax.ppermute(ys, "ctx", flow_pairs(shifts, count)) for shifts in steps]
     x1r = lax.ppermute(x1s, "ctx", across)
     mates = [(i, i ^ 1) for i in range(count)]
     i1r = lax.ppermute(i1s, "ctx", mates)
-    edge_r, i1r = lax.optimization_barrier((edge_r, i1r))
-    via_r = edge_r
-    if detours:
-        via_r = lax.ppermute(edge_r, "ctx", [(via, t) for (_, t), via in detours.items()])
 
     def head(rows, base=0):
         return pl.BlockSpec((rows, head_size), lambda h, *_: (0, base + h))
@@ -449,11 +469,17 @@
         [(key_rows, value_rows), l1, i1r],
         (),
     )
+    edge_r, l4, stats = lax.optimization_barrier((edge_r, l4, stats))
+    via_r = edge_r
+    if detours:
+        via_r = lax.ppermute(edge_r, "ctx", [(via, t) for (_, t), via in detours.items()])
+    steps = [shifts for shifts in flow_spans if abs(shifts[0]) != 4]
+    yrs += [lax.ppermute(l4, "ctx", flow_pairs(shifts, count)) for shifts in steps]
     x2r, yrs, stats = lax.optimization_barrier((x2r, yrs, stats))
     tables = [x2r, lax.ppermute(x2r, "ctx", mates)]
     for yr in yrs:
         tables += [yr, lax.ppermute(yr, "ctx", mates)]
-    edge_r, via_r, x1r, stats = lax.optimization_barrier((edge_r, via_r, x1r, stats))
+    edge_r, via_r, x1r, tables = lax.optimization_barrier((edge_r, via_r, x1r, tables))
     xt, i2s = pl.pallas_call(
         functools.partial(rim_kernel, [t for _, t in detours]),
         name="rim",

time: 57.1 us -> 54.8 us (0.960)
  the two profiles are of different devices: /device:TPU:27 before, /device:TPU:0 now
where the time goes in v3:
time: 54.8 us; the launch traced here: 54.5 us
  Pallas kernels  27.6 us (50%)
  starting transfers between devices  19 us (35%)
  waiting for transfers between devices  6.87 us (13%)
  local copies, waits for them, and re-layouts  0.79 us (1%)
    pallas_call x2, Pallas kernels, attention(): pl.pallas_call(kernel, name=name, grid=(HEADS,), out_shape=shape(token_ro...  20.2 us
    ppermute x1, starting transfers between devices, on_device(): lax.ppermute(x2s, 'ctx', [(i, i + 3) for i in range(0, count - 3, 2)] + [...  7.15 us
    pallas_call x1, Pallas kernels, on_device(): pl.pallas_call(pool_kernel, name='pool', grid=(2,), out_shape=[shape(rows...  4.52 us
    ppermute x1, starting transfers between devices, on_device(): lax.ppermute(l4, 'ctx', flow_pairs(shifts, count))  4.34 us
    ppermute x1, waiting for transfers between devices, on_device(): lax.ppermute(l4, 'ctx', flow_pairs(shifts, count))  2.89 us
    pallas_call x1, Pallas kernels, on_device(): pl.pallas_call(functools.partial(rim_kernel, [t for _, t in detours]), na...  2.82 us
    ppermute x1, starting transfers between devices, on_device(): lax.ppermute(edge_r, 'ctx', [(via, t) for (_, t), via in detours.items()])  2.1 us
    ppermute x1, waiting for transfers between devices, on_device(): i2r = lax.ppermute(i2s, 'ctx', mates)  1.88 us
  transfers between devices with their start and end apart: 11, of which 4 were waited for; matrix products, arithmetic and copies ran while one was open for 0% of the time, Pallas kernels for 19%

profile of v3, /device:TPU:0, one launch (start us, length us, event | category | flops | bytes accessed | tf_op | source)
XLA Modules:
  0.0 54.5 jit_solution(1458531501371115630)
XLA Ops:
  0.0 4.5 %pool.1 = (bf16[256,1024]{1,0:T(8,128)(2,1)}, bf16[320,1024]{1,0:T(8,128)(2,1)}, bf16[896,1024]{1,0:T(8,128)(2,1)}, bf16[192,1024]{1,0:T(8,128)(2,1)}, bf16[192,...) custom-call(s32[1]{0:T(128)} %bitcast.dev_ref, bf16[1024,512]{1,0:T(8,128)(2,1)} %k_ref.3, ...), custom_call_target="tpu_custom_call" | custom-call | bytes 25165824 | tf_op jit(solution)/shard_map/pool/pallas_call | solution.py:407
  4.5 0.5 collective-permute-start.1
  5.0 1.3 %collective-permute-start = (bf16[256,1024]{1,0:T(8,128)(2,1)}, bf16[256,1024]{1,0:T(8,128)(2,1)}, u32[]{:S(2)}, u32[]{:S(2)}) collective-permute-start(bf16[256,1024]{1,0:T(8,128)(2,1)} %get-tuple-element.34), channel_id=1, source_target_pairs={{4,8},{12,28},{20,24},{8,4},{16,0},{24,20},{5,9},{13,29},{21,25},{... | collective-permute-start | bytes 1572872 | tf_op jit(solution)/shard_map/ppermute | solution.py:423
  6.3 7.2 %collective-permute-start.4 = (bf16[192,1024]{1,0:T(8,128)(2,1)}, bf16[192,1024]{1,0:T(8,128)(2,1)}, u32[]{:S(2)}, u32[]{:S(2)}) collective-permute-start(bf16[192,1024]{1,0:T(8,128)(2,1)} %get-tuple-element.42), channel_id=1, source_target_pairs={{0,12},{8,20},{16,28},{12,0},{20,8},{28,16},{1,13},{9,21},{17,29},... | collective-permute-start | bytes 1179656 | tf_op jit(solution)/shard_map/ppermute | solution.py:424
  13.5 0.1 collective-permute-start.5
  13.5 1.5 %collective-permute-start.3 = (bf16[320,1024]{1,0:T(8,128)(2,1)}, bf16[320,1024]{1,0:T(8,128)(2,1)}, u32[]{:S(2)}, u32[]{:S(2)}) collective-permute-start(bf16[320,1024]{1,0:T(8,128)(2,1)} %get-tuple-element.41), channel_id=1, source_target_pairs={{4,8},{12,16},{20,24},{8,4},{16,12},{24,20},{5,9},{13,17},{21,25},... | collective-permute-start | bytes 1966088 | tf_op jit(solution)/shard_map/ppermute | solution.py:432
  15.1 0.0 collective-permute-done.1.mk.mv
  15.1 10.5 %near.1 = (f32[1024,512]{1,0:T(8,128)}, f32[1024,128]{1,0:T(8,128)}) custom-call(s32[1]{0:T(128)} %bitcast.dev_ref, bf16[1024,512]{1,0:T(8,128)(2,1)} %q_ref.3, bf16[1024,512]{1,0:T(8,128)(2,1)} %k_ref.3, bf16[1024,512]{1,0:T(8,128)(2,1)} %v_ref.3, bf16[512,1024]{1,0:T(8,128)(2,1)} %get-tuple-element.36.l1k.l1v, ...), custom_call_target="tpu_custom_call" | custom-call | flops 2415919104 | bytes 12582912 | tf_op jit(solution)/shard_map/near/pallas_call | solution.py:451
  25.6 0.0 collective-permute-done.edge_ref
  25.6 4.3 %collective-permute-start.6 = (bf16[64,1024]{1,0:T(8,128)(2,1)}, bf16[64,1024]{1,0:T(8,128)(2,1)S(1)}, u32[]{:S(2)}, u32[]{:S(2)}) collective-permute-start(bf16[64,1024]{1,0:T(8,128)(2,1)} %get-tuple-element.44), channel_id=1, source_target_pairs={{24,0},{28,4},{0,24},{4,28},{25,1},{29,5},{1,25},{5,29},{26,2},{30... | collective-permute-start | bytes 393224 | tf_op jit(solution)/shard_map/ppermute | solution.py:477
  30.0 2.1 %collective-permute-start.2 = (bf16[256,1024]{1,0:T(8,128)(2,1)}, bf16[256,1024]{1,0:T(8,128)(2,1)}, u32[]{:S(2)}, u32[]{:S(2)}) collective-permute-start(bf16[256,1024]{1,0:T(8,128)(2,1)} %collective-permute-done.edge_ref), channel_id=1, source_target_pairs={{28,16},{0,12},{29,17},{1,13},{30,18},{2,14},{31,19},{3,15}} | collective-permute-start | bytes 1572872 | tf_op jit(solution)/shard_map/ppermute | solution.py:475
  32.1 2.9 %collective-permute-done.6.refs_12_.refs_13_ = bf16[64,1024]{1,0:T(8,128)(2,1)S(1)} collective-permute-done((bf16[64,1024]{1,0:T(8,128)(2,1)}, bf16[64,1024]{1,0:T(8,128)(2,1)S(1)}, u32[]{:S(2)}, u32[]{:S(2)}) %collective-permute-start.6) | collective-permute-done | bytes 131104 | tf_op jit(solution)/shard_map/ppermute | solution.py:477
  35.0 0.0 collective-permute-start.7
  35.0 0.5 collective-permute-start.8
  35.5 0.1 copy-done
  35.6 0.0 collective-permute-start.9
  35.6 0.0 collective-permute-done.3.x1_ref
  35.6 1.8 %collective-permute-done.9.refs_14_.refs_15_ = bf16[64,1024]{1,0:T(8,128)(2,1)S(1)} collective-permute-done((bf16[64,1024]{1,0:T(8,128)(2,1)S(1)}, bf16[64,1024]{1,0:T(8,128)(2,1)S(1)}, u32[]{:S(2)}, u32[]{:S(2)}) %collective-permute-start.9) | collective-permute-done | bytes 131104 | tf_op jit(solution)/shard_map/ppermute | solution.py:481
  37.4 0.7 %copy-done.1 = bf16[64,1024]{1,0:T(8,128)(2,1)} copy-done((bf16[64,1024]{1,0:T(8,128)(2,1)}, bf16[64,1024]{1,0:T(8,128)(2,1)S(1)}, u32[]{:S(2)}) %copy-start.1) | copy-done | bytes 131096
  38.1 0.3 collective-permute-done.2.via_ref
  38.4 2.8 %rim.1 = (bf16[896,1024]{1,0:T(8,128)(2,1)}, bf16[256,1024]{1,0:T(8,128)(2,1)}) custom-call(s32[1]{0:T(128)} %bitcast.dev_ref, bf16[256,1024]{1,0:T(8,128)(2,1)} %collective-permute-done.edge_ref, bf16[256,1024]{1,0:T(8,128)(2,1)} %collective-permute-done.2.via_ref, bf16[320,1024]{1,0:T(8,128)(2,1)} %collective-permute-done.3.x1_ref), custom_call_target="tpu_custom_call" | custom-call | tf_op jit(solution)/shard_map/rim/pallas_call | solution.py:483
  41.2 1.6 %collective-permute-start.10 = (bf16[256,1024]{1,0:T(8,128)(2,1)}, bf16[256,1024]{1,0:T(8,128)(2,1)}, u32[]{:S(2)}, u32[]{:S(2)}) collective-permute-start(bf16[256,1024]{1,0:T(8,128)(2,1)} %get-tuple-element.54), channel_id=1, source_target_pairs={{0,4},{4,0},{8,12},{12,8},{16,20},{20,16},{24,28},{28,24},{1,5},{5... | collective-permute-start | bytes 1572872 | tf_op jit(solution)/shard_map/ppermute | solution.py:493
  42.8 1.9 %collective-permute-done.10.refs_2_.refs_3_ = bf16[256,1024]{1,0:T(8,128)(2,1)} collective-permute-done((bf16[256,1024]{1,0:T(8,128)(2,1)}, bf16[256,1024]{1,0:T(8,128)(2,1)}, u32[]{:S(2)}, u32[]{:S(2)}) %collective-permute-start.10) | collective-permute-done | bytes 524320 | tf_op jit(solution)/shard_map/ppermute | solution.py:493
  44.6 9.7 %far.1 = bf16[1024,512]{1,0:T(8,128)(2,1)} custom-call(s32[1]{0:T(128)} %bitcast.dev_ref, bf16[1024,512]{1,0:T(8,128)(2,1)} %q_ref.3, bf16[896,1024]{1,0:T(8,128)(2,1)} %get-tuple-element.53.refs_0_.refs_1_, bf16[896,1024]{1,0:T(8,128)(2,1)} %get-tuple-element.53.refs_0_.refs_1_, bf16[256,1024]{1,0:T(8,128)(2,1)} %collective-permute-done.10.refs_2_.refs_3_, ...), custom_call_target="tpu_custom_call" | custom-call | flops 2281701376 | bytes 12582912 | tf_op jit(solution)/shard_map/far/pallas_call | solution.py:451
  (6 shorter events, 0.0 us)
Async XLA Ops:
  4.5 10.5 %collective-permute-start.1 = (bf16[896,1024]{1,0:T(8,128)(2,1)}, bf16[896,1024]{1,0:T(8,128)(2,1)}, u32[]{:S(2)}, u32[]{:S(2)}) collective-permute-start(bf16[896,1024]{1,0:T(8,128)(2,1)} %get-tuple-element.37), channel_id=1, source_target_pairs={{0,4},{4,0},{8,12},{12,8},{16,20},{20,16},{24,28},{28,24},{1,5},{5... | collective-permute-start | bytes 5505032 | tf_op jit(solution)/shard_map/ppermute | solution.py:434
  5.0 20.6 %collective-permute-start = (bf16[256,1024]{1,0:T(8,128)(2,1)}, bf16[256,1024]{1,0:T(8,128)(2,1)}, u32[]{:S(2)}, u32[]{:S(2)}) collective-permute-start(bf16[256,1024]{1,0:T(8,128)(2,1)} %get-tuple-element.34), channel_id=1, source_target_pairs={{4,8},{12,28},{20,24},{8,4},{16,0},{24,20},{5,9},{13,29},{21,25},{... | collective-permute-start | bytes 1572872 | tf_op jit(solution)/shard_map/ppermute | solution.py:423
  6.3 25.8 %collective-permute-start.4 = (bf16[192,1024]{1,0:T(8,128)(2,1)}, bf16[192,1024]{1,0:T(8,128)(2,1)}, u32[]{:S(2)}, u32[]{:S(2)}) collective-permute-start(bf16[192,1024]{1,0:T(8,128)(2,1)} %get-tuple-element.42), channel_id=1, source_target_pairs={{0,12},{8,20},{16,28},{12,0},{20,8},{28,16},{1,13},{9,21},{17,29},... | collective-permute-start | bytes 1179656 | tf_op jit(solution)/shard_map/ppermute | solution.py:424
  13.5 18.6 %collective-permute-start.5 = (bf16[192,1024]{1,0:T(8,128)(2,1)}, bf16[192,1024]{1,0:T(8,128)(2,1)}, u32[]{:S(2)}, u32[]{:S(2)}) collective-permute-start(bf16[192,1024]{1,0:T(8,128)(2,1)} %get-tuple-element.43), channel_id=1, source_target_pairs={{16,0},{20,4},{24,8},{28,12},{0,16},{4,20},{8,24},{12,28},{17,1},{... | collective-permute-start | bytes 1179656 | tf_op jit(solution)/shard_map/ppermute | solution.py:431
  13.5 22.1 %collective-permute-start.3 = (bf16[320,1024]{1,0:T(8,128)(2,1)}, bf16[320,1024]{1,0:T(8,128)(2,1)}, u32[]{:S(2)}, u32[]{:S(2)}) collective-permute-start(bf16[320,1024]{1,0:T(8,128)(2,1)} %get-tuple-element.41), channel_id=1, source_target_pairs={{4,8},{12,16},{20,24},{8,4},{16,12},{24,20},{5,9},{13,17},{21,25},... | collective-permute-start | bytes 1966088 | tf_op jit(solution)/shard_map/ppermute | solution.py:432
  25.6 9.3 %collective-permute-start.6 = (bf16[64,1024]{1,0:T(8,128)(2,1)}, bf16[64,1024]{1,0:T(8,128)(2,1)S(1)}, u32[]{:S(2)}, u32[]{:S(2)}) collective-permute-start(bf16[64,1024]{1,0:T(8,128)(2,1)} %get-tuple-element.44), channel_id=1, source_target_pairs={{24,0},{28,4},{0,24},{4,28},{25,1},{29,5},{1,25},{5,29},{26,2},{30... | collective-permute-start | bytes 393224 | tf_op jit(solution)/shard_map/ppermute | solution.py:477
  30.0 8.4 %collective-permute-start.2 = (bf16[256,1024]{1,0:T(8,128)(2,1)}, bf16[256,1024]{1,0:T(8,128)(2,1)}, u32[]{:S(2)}, u32[]{:S(2)}) collective-permute-start(bf16[256,1024]{1,0:T(8,128)(2,1)} %collective-permute-done.edge_ref), channel_id=1, source_target_pairs={{28,16},{0,12},{29,17},{1,13},{30,18},{2,14},{31,19},{3,15}} | collective-permute-start | bytes 1572872 | tf_op jit(solution)/shard_map/ppermute | solution.py:475
  35.0 0.6 %copy-start = (bf16[64,1024]{1,0:T(8,128)(2,1)}, bf16[64,1024]{1,0:T(8,128)(2,1)S(1)}, u32[]{:S(2)}) copy-start(bf16[64,1024]{1,0:T(8,128)(2,1)S(1)} %collective-permute-done.6.refs_12_.refs_13_) | copy-start | bytes 393220
  35.0 3.1 %collective-permute-start.7 = (bf16[192,1024]{1,0:T(8,128)(2,1)}, bf16[192,1024]{1,0:T(8,128)(2,1)}, u32[]{:S(2)}, u32[]{:S(2)}) collective-permute-start(bf16[192,1024]{1,0:T(8,128)(2,1)} %collective-permute-done.4.refs_4_.refs_5_), channel_id=1, source_target_pairs={{0,4},{4,0},{8,12},{12,8},{16,20},{20,16},{24,28},{28,24},{1,5},{5... | collective-permute-start | bytes 1179656 | tf_op jit(solution)/shard_map/ppermute | solution.py:479
  35.0 3.1 %collective-permute-start.8 = (bf16[192,1024]{1,0:T(8,128)(2,1)}, bf16[192,1024]{1,0:T(8,128)(2,1)}, u32[]{:S(2)}, u32[]{:S(2)}) collective-permute-start(bf16[192,1024]{1,0:T(8,128)(2,1)} %collective-permute-done.5.refs_8_.refs_9_), channel_id=1, source_target_pairs={{0,4},{4,0},{8,12},{12,8},{16,20},{20,16},{24,28},{28,24},{1,5},{5... | collective-permute-start | bytes 1179656 | tf_op jit(solution)/shard_map/ppermute | solution.py:481
  35.6 1.8 %collective-permute-start.9 = (bf16[64,1024]{1,0:T(8,128)(2,1)S(1)}, bf16[64,1024]{1,0:T(8,128)(2,1)S(1)}, u32[]{:S(2)}, u32[]{:S(2)}) collective-permute-start(bf16[64,1024]{1,0:T(8,128)(2,1)S(1)} %collective-permute-done.6.refs_12_.refs_13_), channel_id=1, source_target_pairs={{0,4},{4,0},{8,12},{12,8},{16,20},{20,16},{24,28},{28,24},{1,5},{5... | collective-permute-start | bytes 393224 | tf_op jit(solution)/shard_map/ppermute | solution.py:481
  37.4 0.7 %copy-start.1 = (bf16[64,1024]{1,0:T(8,128)(2,1)}, bf16[64,1024]{1,0:T(8,128)(2,1)S(1)}, u32[]{:S(2)}) copy-start(bf16[64,1024]{1,0:T(8,128)(2,1)S(1)} %collective-permute-done.9.refs_14_.refs_15_) | copy-start | bytes 393220
  41.2 3.4 %collective-permute-start.10 = (bf16[256,1024]{1,0:T(8,128)(2,1)}, bf16[256,1024]{1,0:T(8,128)(2,1)}, u32[]{:S(2)}, u32[]{:S(2)}) collective-permute-start(bf16[256,1024]{1,0:T(8,128)(2,1)} %get-tuple-element.54), channel_id=1, source_target_pairs={{0,4},{4,0},{8,12},{12,8},{16,20},{20,16},{24,28},{28,24},{1,5},{5... | collective-permute-start | bytes 1572872 | tf_op jit(solution)/shard_map/ppermute | solution.py:493

commit v4 on v3

--- a/solution.py
+++ b/solution.py
@@ -427,8 +427,10 @@
         [(i, i + 3) for i in range(0, count - 3, 2)] + [(i, i - 3) for i in range(3, count, 2)],
     )
     flow_spans = far_flows(count)
-    steps = [shifts for shifts in flow_spans if abs(shifts[0]) == 4]
-    yrs = [lax.ppermute(ys, "ctx", flow_pairs(shifts, count)) for shifts in steps]
+    yrs = [
+        lax.ppermute(ys if abs(shifts[0]) == 4 else l4, "ctx", flow_pairs(shifts, count))
+        for shifts in flow_spans
+    ]
     x1r = lax.ppermute(x1s, "ctx", across)
     mates = [(i, i ^ 1) for i in range(count)]
     i1r = lax.ppermute(i1s, "ctx", mates)
@@ -469,12 +471,10 @@
         [(key_rows, value_rows), l1, i1r],
         (),
     )
-    edge_r, l4, stats = lax.optimization_barrier((edge_r, l4, stats))
+    edge_r, stats = lax.optimization_barrier((edge_r, stats))
     via_r = edge_r
     if detours:
         via_r = lax.ppermute(edge_r, "ctx", [(via, t) for (_, t), via in detours.items()])
-    steps = [shifts for shifts in flow_spans if abs(shifts[0]) != 4]
-    yrs += [lax.ppermute(l4, "ctx", flow_pairs(shifts, count)) for shifts in steps]
     x2r, yrs, stats = lax.optimization_barrier((x2r, yrs, stats))
     tables = [x2r, lax.ppermute(x2r, "ctx", mates)]
     for yr in yrs:

time: 54.8 us -> 54.4 us (level)
  local copies, waits for them, and re-layouts: 0.79 us -> 0 us
  waiting for transfers between devices: 6.87 us -> 7.42 us
    ppermute x1, waiting for transfers between devices: 0.27 us -> 3.3 us  [on_device(): lax.ppermute(edge_r, 'ctx', [(via, t) for (_, t), via in detours.items()])]
    ppermute x2, waiting for transfers between devices: 2.89 us -> 0.01 us  [on_device(): lax.ppermute(ys if abs(shifts[0]) == 4 else l4, 'ctx', flow_pairs(shifts,...]
    unnamed x4 -> x0, local copies, waits for them, and re-layouts: 0.79 us -> none
    ppermute x1, starting transfers between devices: 1.57 us -> 0.81 us  [on_device(): i2r = lax.ppermute(i2s, 'ctx', mates)]
    ppermute x1, starting transfers between devices: 2.1 us -> 2.77 us  [on_device(): lax.ppermute(edge_r, 'ctx', [(via, t) for (_, t), via in detours.items()])]
  transfers between devices with their start and end apart: 11 -> 11, of which waited for: 4 -> 3; matrix products, arithmetic and copies ran while one was open for 0% -> 0% of each run, Pallas kernels for 19% -> 20%
where the time goes in v4:
time: 54.4 us; the launch traced here: 53.8 us
  Pallas kernels  27.5 us (51%)
  starting transfers between devices  18.7 us (34%)
  waiting for transfers between devices  7.42 us (14%)
    pallas_call x2, Pallas kernels, attention(): pl.pallas_call(kernel, name=name, grid=(HEADS,), out_shape=shape(token_ro...  20.2 us
    ppermute x1, starting transfers between devices, on_device(): lax.ppermute(x2s, 'ctx', [(i, i + 3) for i in range(0, count - 3, 2)] + [...  7.14 us
    pallas_call x1, Pallas kernels, on_device(): pl.pallas_call(pool_kernel, name='pool', grid=(2,), out_shape=[shape(rows...  4.52 us
    ppermute x2, starting transfers between devices, on_device(): lax.ppermute(ys if abs(shifts[0]) == 4 else l4, 'ctx', flow_pairs(shifts,...  3.99 us
    ppermute x1, waiting for transfers between devices, on_device(): lax.ppermute(edge_r, 'ctx', [(via, t) for (_, t), via in detours.items()])  3.3 us
    pallas_call x1, Pallas kernels, on_device(): pl.pallas_call(functools.partial(rim_kernel, [t for _, t in detours]), na...  2.82 us
    ppermute x1, starting transfers between devices, on_device(): lax.ppermute(edge_r, 'ctx', [(via, t) for (_, t), via in detours.items()])  2.77 us
    ppermute x2, waiting for transfers between devices, on_device(): tables += [yr, lax.ppermute(yr, 'ctx', mates)]  2.22 us
  transfers between devices with their start and end apart: 11, of which 3 were waited for; matrix products, arithmetic and copies ran while one was open for 0% of the time, Pallas kernels for 20%

profile of v4, /device:TPU:0, one launch (start us, length us, event | category | flops | bytes accessed | tf_op | source)
XLA Modules:
  0.0 53.8 jit_solution(13863799949188955989)
XLA Ops:
  0.0 4.5 %pool.1 = (bf16[256,1024]{1,0:T(8,128)(2,1)}, bf16[320,1024]{1,0:T(8,128)(2,1)}, bf16[896,1024]{1,0:T(8,128)(2,1)}, bf16[192,1024]{1,0:T(8,128)(2,1)}, bf16[192,...) custom-call(s32[1]{0:T(128)} %bitcast.dev_ref, bf16[1024,512]{1,0:T(8,128)(2,1)} %k_ref.3, ...), custom_call_target="tpu_custom_call" | custom-call | bytes 25165824 | tf_op jit(solution)/shard_map/pool/pallas_call | solution.py:407
  4.5 0.5 collective-permute-start.1
  5.0 1.3 %collective-permute-start = (bf16[256,1024]{1,0:T(8,128)(2,1)}, bf16[256,1024]{1,0:T(8,128)(2,1)}, u32[]{:S(2)}, u32[]{:S(2)}) collective-permute-start(bf16[256,1024]{1,0:T(8,128)(2,1)} %get-tuple-element.33), channel_id=1, source_target_pairs={{4,8},{12,28},{20,24},{8,4},{16,0},{24,20},{5,9},{13,29},{21,25},{... | collective-permute-start | bytes 1572872 | tf_op jit(solution)/shard_map/ppermute | solution.py:423
  6.3 7.1 %collective-permute-start.4 = (bf16[192,1024]{1,0:T(8,128)(2,1)}, bf16[192,1024]{1,0:T(8,128)(2,1)}, u32[]{:S(2)}, u32[]{:S(2)}) collective-permute-start(bf16[192,1024]{1,0:T(8,128)(2,1)} %get-tuple-element.40), channel_id=1, source_target_pairs={{0,12},{8,20},{16,28},{12,0},{20,8},{28,16},{1,13},{9,21},{17,29},... | collective-permute-start | bytes 1179656 | tf_op jit(solution)/shard_map/ppermute | solution.py:424
  13.5 0.1 collective-permute-start.5
  13.5 3.9 %collective-permute-start.6 = (bf16[64,1024]{1,0:T(8,128)(2,1)}, bf16[64,1024]{1,0:T(8,128)(2,1)}, u32[]{:S(2)}, u32[]{:S(2)}) collective-permute-start(bf16[64,1024]{1,0:T(8,128)(2,1)} %get-tuple-element.42), channel_id=1, source_target_pairs={{24,0},{28,4},{0,24},{4,28},{25,1},{29,5},{1,25},{5,29},{26,2},{30... | collective-permute-start | bytes 393224 | tf_op jit(solution)/shard_map/ppermute | solution.py:431
  17.5 0.0 collective-permute-done.1.mk.mv
  17.5 1.5 %collective-permute-start.3 = (bf16[320,1024]{1,0:T(8,128)(2,1)}, bf16[320,1024]{1,0:T(8,128)(2,1)}, u32[]{:S(2)}, u32[]{:S(2)}) collective-permute-start(bf16[320,1024]{1,0:T(8,128)(2,1)} %get-tuple-element.39), channel_id=1, source_target_pairs={{4,8},{12,16},{20,24},{8,4},{16,12},{24,20},{5,9},{13,17},{21,25},... | collective-permute-start | bytes 1966088 | tf_op jit(solution)/shard_map/ppermute | solution.py:434
  19.0 10.5 %near.1 = (f32[1024,512]{1,0:T(8,128)}, f32[1024,128]{1,0:T(8,128)}) custom-call(s32[1]{0:T(128)} %bitcast.dev_ref, bf16[1024,512]{1,0:T(8,128)(2,1)} %q_ref.3, bf16[1024,512]{1,0:T(8,128)(2,1)} %k_ref.3, bf16[1024,512]{1,0:T(8,128)(2,1)} %v_ref.3, bf16[512,1024]{1,0:T(8,128)(2,1)} %get-tuple-element.34.l1k.l1v, ...), custom_call_target="tpu_custom_call" | custom-call | flops 2415919104 | bytes 12582912 | tf_op jit(solution)/shard_map/near/pallas_call | solution.py:453
  29.5 2.8 %collective-permute-start.2 = (bf16[256,1024]{1,0:T(8,128)(2,1)}, bf16[256,1024]{1,0:T(8,128)(2,1)}, u32[]{:S(2)}, u32[]{:S(2)}) collective-permute-start(bf16[256,1024]{1,0:T(8,128)(2,1)} %collective-permute-done.edge_ref), channel_id=1, source_target_pairs={{28,16},{0,12},{29,17},{1,13},{30,18},{2,14},{31,19},{3,15}} | collective-permute-start | bytes 1572872 | tf_op jit(solution)/shard_map/ppermute | solution.py:477
  32.3 0.0 collective-permute-done.6.refs_12_.refs_13_
  32.3 0.0 collective-permute-done.4.refs_4_.refs_5_
  32.3 0.0 collective-permute-done.5.refs_8_.refs_9_
  32.3 0.1 collective-permute-start.7
  32.4 0.5 collective-permute-start.8
  32.9 0.1 collective-permute-start.9
  32.9 0.0 collective-permute-done.3.x1_ref
  32.9 2.2 %collective-permute-done.9.refs_14_.refs_15_ = bf16[64,1024]{1,0:T(8,128)(2,1)} collective-permute-done((bf16[64,1024]{1,0:T(8,128)(2,1)}, bf16[64,1024]{1,0:T(8,128)(2,1)}, u32[]{:S(2)}, u32[]{:S(2)}) %collective-permute-start.9) | collective-permute-done | bytes 131104 | tf_op jit(solution)/shard_map/ppermute | solution.py:481
  35.2 0.0 collective-permute-done.7.refs_6_.refs_7_
  35.2 3.3 %collective-permute-done.2.via_ref = bf16[256,1024]{1,0:T(8,128)(2,1)} collective-permute-done((bf16[256,1024]{1,0:T(8,128)(2,1)}, bf16[256,1024]{1,0:T(8,128)(2,1)}, u32[]{:S(2)}, u32[]{:S(2)}) %collective-permute-start.2) | collective-permute-done | bytes 524320 | tf_op jit(solution)/shard_map/ppermute | solution.py:477
  38.5 2.8 %rim.1 = (bf16[896,1024]{1,0:T(8,128)(2,1)}, bf16[256,1024]{1,0:T(8,128)(2,1)}) custom-call(s32[1]{0:T(128)} %bitcast.dev_ref, bf16[256,1024]{1,0:T(8,128)(2,1)} %collective-permute-done.edge_ref, bf16[256,1024]{1,0:T(8,128)(2,1)} %collective-permute-done.2.via_ref, bf16[320,1024]{1,0:T(8,128)(2,1)} %collective-permute-done.3.x1_ref), custom_call_target="tpu_custom_call" | custom-call | tf_op jit(solution)/shard_map/rim/pallas_call | solution.py:483
  41.3 0.8 %collective-permute-start.10 = (bf16[256,1024]{1,0:T(8,128)(2,1)}, bf16[256,1024]{1,0:T(8,128)(2,1)}, u32[]{:S(2)}, u32[]{:S(2)}) collective-permute-start(bf16[256,1024]{1,0:T(8,128)(2,1)} %get-tuple-element.52), channel_id=1, source_target_pairs={{0,4},{4,0},{8,12},{12,8},{16,20},{20,16},{24,28},{28,24},{1,5},{5... | collective-permute-start | bytes 1572872 | tf_op jit(solution)/shard_map/ppermute | solution.py:493
  42.1 1.9 %collective-permute-done.10.refs_2_.refs_3_ = bf16[256,1024]{1,0:T(8,128)(2,1)} collective-permute-done((bf16[256,1024]{1,0:T(8,128)(2,1)}, bf16[256,1024]{1,0:T(8,128)(2,1)}, u32[]{:S(2)}, u32[]{:S(2)}) %collective-permute-start.10) | collective-permute-done | bytes 524320 | tf_op jit(solution)/shard_map/ppermute | solution.py:493
  44.0 9.7 %far.1 = bf16[1024,512]{1,0:T(8,128)(2,1)} custom-call(s32[1]{0:T(128)} %bitcast.dev_ref, bf16[1024,512]{1,0:T(8,128)(2,1)} %q_ref.3, bf16[896,1024]{1,0:T(8,128)(2,1)} %get-tuple-element.51.refs_0_.refs_1_, bf16[896,1024]{1,0:T(8,128)(2,1)} %get-tuple-element.51.refs_0_.refs_1_, bf16[256,1024]{1,0:T(8,128)(2,1)} %collective-permute-done.10.refs_2_.refs_3_, ...), custom_call_target="tpu_custom_call" | custom-call | flops 2281701376 | bytes 12582912 | tf_op jit(solution)/shard_map/far/pallas_call | solution.py:453
  (2 shorter events, 0.0 us)
Async XLA Ops:
  4.5 12.9 %collective-permute-start.1 = (bf16[896,1024]{1,0:T(8,128)(2,1)}, bf16[896,1024]{1,0:T(8,128)(2,1)}, u32[]{:S(2)}, u32[]{:S(2)}) collective-permute-start(bf16[896,1024]{1,0:T(8,128)(2,1)} %get-tuple-element.35), channel_id=1, source_target_pairs={{0,4},{4,0},{8,12},{12,8},{16,20},{20,16},{24,28},{28,24},{1,5},{5... | collective-permute-start | bytes 5505032 | tf_op jit(solution)/shard_map/ppermute | solution.py:436
  5.0 24.5 %collective-permute-start = (bf16[256,1024]{1,0:T(8,128)(2,1)}, bf16[256,1024]{1,0:T(8,128)(2,1)}, u32[]{:S(2)}, u32[]{:S(2)}) collective-permute-start(bf16[256,1024]{1,0:T(8,128)(2,1)} %get-tuple-element.33), channel_id=1, source_target_pairs={{4,8},{12,28},{20,24},{8,4},{16,0},{24,20},{5,9},{13,29},{21,25},{... | collective-permute-start | bytes 1572872 | tf_op jit(solution)/shard_map/ppermute | solution.py:423
  6.3 26.0 %collective-permute-start.4 = (bf16[192,1024]{1,0:T(8,128)(2,1)}, bf16[192,1024]{1,0:T(8,128)(2,1)}, u32[]{:S(2)}, u32[]{:S(2)}) collective-permute-start(bf16[192,1024]{1,0:T(8,128)(2,1)} %get-tuple-element.40), channel_id=1, source_target_pairs={{0,12},{8,20},{16,28},{12,0},{20,8},{28,16},{1,13},{9,21},{17,29},... | collective-permute-start | bytes 1179656 | tf_op jit(solution)/shard_map/ppermute | solution.py:424
  13.5 18.8 %collective-permute-start.5 = (bf16[192,1024]{1,0:T(8,128)(2,1)}, bf16[192,1024]{1,0:T(8,128)(2,1)}, u32[]{:S(2)}, u32[]{:S(2)}) collective-permute-start(bf16[192,1024]{1,0:T(8,128)(2,1)} %get-tuple-element.41), channel_id=1, source_target_pairs={{16,0},{20,4},{24,8},{28,12},{0,16},{4,20},{8,24},{12,28},{17,1},{... | collective-permute-start | bytes 1179656 | tf_op jit(solution)/shard_map/ppermute | solution.py:431
  13.5 18.7 %collective-permute-start.6 = (bf16[64,1024]{1,0:T(8,128)(2,1)}, bf16[64,1024]{1,0:T(8,128)(2,1)}, u32[]{:S(2)}, u32[]{:S(2)}) collective-permute-start(bf16[64,1024]{1,0:T(8,128)(2,1)} %get-tuple-element.42), channel_id=1, source_target_pairs={{24,0},{28,4},{0,24},{4,28},{25,1},{29,5},{1,25},{5,29},{26,2},{30... | collective-permute-start | bytes 393224 | tf_op jit(solution)/shard_map/ppermute | solution.py:431
  17.5 15.5 %collective-permute-start.3 = (bf16[320,1024]{1,0:T(8,128)(2,1)}, bf16[320,1024]{1,0:T(8,128)(2,1)}, u32[]{:S(2)}, u32[]{:S(2)}) collective-permute-start(bf16[320,1024]{1,0:T(8,128)(2,1)} %get-tuple-element.39), channel_id=1, source_target_pairs={{4,8},{12,16},{20,24},{8,4},{16,12},{24,20},{5,9},{13,17},{21,25},... | collective-permute-start | bytes 1966088 | tf_op jit(solution)/shard_map/ppermute | solution.py:434
  29.5 9.0 %collective-permute-start.2 = (bf16[256,1024]{1,0:T(8,128)(2,1)}, bf16[256,1024]{1,0:T(8,128)(2,1)}, u32[]{:S(2)}, u32[]{:S(2)}) collective-permute-start(bf16[256,1024]{1,0:T(8,128)(2,1)} %collective-permute-done.edge_ref), channel_id=1, source_target_pairs={{28,16},{0,12},{29,17},{1,13},{30,18},{2,14},{31,19},{3,15}} | collective-permute-start | bytes 1572872 | tf_op jit(solution)/shard_map/ppermute | solution.py:477
  32.3 2.9 %collective-permute-start.7 = (bf16[192,1024]{1,0:T(8,128)(2,1)}, bf16[192,1024]{1,0:T(8,128)(2,1)}, u32[]{:S(2)}, u32[]{:S(2)}) collective-permute-start(bf16[192,1024]{1,0:T(8,128)(2,1)} %collective-permute-done.4.refs_4_.refs_5_), channel_id=1, source_target_pairs={{0,4},{4,0},{8,12},{12,8},{16,20},{20,16},{24,28},{28,24},{1,5},{5... | collective-permute-start | bytes 1179656 | tf_op jit(solution)/shard_map/ppermute | solution.py:479
  32.4 2.8 %collective-permute-start.8 = (bf16[192,1024]{1,0:T(8,128)(2,1)}, bf16[192,1024]{1,0:T(8,128)(2,1)}, u32[]{:S(2)}, u32[]{:S(2)}) collective-permute-start(bf16[192,1024]{1,0:T(8,128)(2,1)} %collective-permute-done.5.refs_8_.refs_9_), channel_id=1, source_target_pairs={{0,4},{4,0},{8,12},{12,8},{16,20},{20,16},{24,28},{28,24},{1,5},{5... | collective-permute-start | bytes 1179656 | tf_op jit(solution)/shard_map/ppermute | solution.py:481
  32.9 2.3 %collective-permute-start.9 = (bf16[64,1024]{1,0:T(8,128)(2,1)}, bf16[64,1024]{1,0:T(8,128)(2,1)}, u32[]{:S(2)}, u32[]{:S(2)}) collective-permute-start(bf16[64,1024]{1,0:T(8,128)(2,1)} %collective-permute-done.6.refs_12_.refs_13_), channel_id=1, source_target_pairs={{0,4},{4,0},{8,12},{12,8},{16,20},{20,16},{24,28},{28,24},{1,5},{5... | collective-permute-start | bytes 393224 | tf_op jit(solution)/shard_map/ppermute | solution.py:481
  41.3 2.7 %collective-permute-start.10 = (bf16[256,1024]{1,0:T(8,128)(2,1)}, bf16[256,1024]{1,0:T(8,128)(2,1)}, u32[]{:S(2)}, u32[]{:S(2)}) collective-permute-start(bf16[256,1024]{1,0:T(8,128)(2,1)} %get-tuple-element.52), channel_id=1, source_target_pairs={{0,4},{4,0},{8,12},{12,8},{16,20},{20,16},{24,28},{28,24},{1,5},{5... | collective-permute-start | bytes 1572872 | tf_op jit(solution)/shard_map/ppermute | solution.py:493

commit v5 on v4

--- a/solution.py
+++ b/solution.py
@@ -260,10 +260,10 @@
 def all_blocks(one_block):
     largest = None
     for block in range(BLOCKS):
-        total = one_block(block, False)
+        total = jnp.max(one_block(block, False), axis=0, keepdims=True)
         largest = total if largest is None else jnp.maximum(largest, total)
 
-    @pl.when(jnp.logical_not(jnp.max(largest) < SAFE_TOTAL))
+    @pl.when(jnp.logical_not(largest[0, 0] < SAFE_TOTAL))
     def _():
         for block in range(BLOCKS):
             one_block(block, True)

time: 54.4 us -> 53.8 us (0.989)
    pallas_call x2, Pallas kernels: 20.2 us -> 19.6 us  [attention(): pl.pallas_call(kernel, name=name, grid=(HEADS,), out_shape=shape(token_ro...]
  transfers between devices with their start and end apart: 11 -> 11, of which waited for: 3 -> 3; matrix products, arithmetic and copies ran while one was open for 0% -> 0% of each run, Pallas kernels for 20% -> 19%
where the time goes in v5:
time: 53.8 us; the launch traced here: 53.5 us
  Pallas kernels  27 us (50%)
  starting transfers between devices  18.9 us (35%)
  waiting for transfers between devices  7.42 us (14%)
    pallas_call x2, Pallas kernels, attention(): pl.pallas_call(kernel, name=name, grid=(HEADS,), out_shape=shape(token_ro...  19.6 us
    ppermute x1, starting transfers between devices, on_device(): lax.ppermute(x2s, 'ctx', [(i, i + 3) for i in range(0, count - 3, 2)] + [...  7.14 us
    pallas_call x1, Pallas kernels, on_device(): pl.pallas_call(pool_kernel, name='pool', grid=(2,), out_shape=[shape(rows...  4.52 us
    ppermute x2, starting transfers between devices, on_device(): lax.ppermute(ys if abs(shifts[0]) == 4 else l4, 'ctx', flow_pairs(shifts,...  3.99 us
    ppermute x1, waiting for transfers between devices, on_device(): lax.ppermute(edge_r, 'ctx', [(via, t) for (_, t), via in detours.items()])  3.3 us
    pallas_call x1, Pallas kernels, on_device(): pl.pallas_call(functools.partial(rim_kernel, [t for _, t in detours]), na...  2.82 us
    ppermute x1, starting transfers between devices, on_device(): lax.ppermute(edge_r, 'ctx', [(via, t) for (_, t), via in detours.items()])  2.73 us
    ppermute x2, waiting for transfers between devices, on_device(): tables += [yr, lax.ppermute(yr, 'ctx', mates)]  2.22 us
  transfers between devices with their start and end apart: 11, of which 3 were waited for; matrix products, arithmetic and copies ran while one was open for 0% of the time, Pallas kernels for 19%

profile of v5, /device:TPU:0, one launch (start us, length us, event | category | flops | bytes accessed | tf_op | source)
XLA Modules:
  0.0 53.5 jit_solution(2977176813035779526)
XLA Ops:
  0.0 4.5 %pool.1 = (bf16[256,1024]{1,0:T(8,128)(2,1)}, bf16[320,1024]{1,0:T(8,128)(2,1)}, bf16[896,1024]{1,0:T(8,128)(2,1)}, bf16[192,1024]{1,0:T(8,128)(2,1)}, bf16[192,...) custom-call(s32[1]{0:T(128)} %bitcast.dev_ref, bf16[1024,512]{1,0:T(8,128)(2,1)} %k_ref.3, ...), custom_call_target="tpu_custom_call" | custom-call | bytes 25165824 | tf_op jit(solution)/shard_map/pool/pallas_call | solution.py:407
  4.5 0.5 collective-permute-start.1
  5.0 1.3 %collective-permute-start = (bf16[256,1024]{1,0:T(8,128)(2,1)}, bf16[256,1024]{1,0:T(8,128)(2,1)}, u32[]{:S(2)}, u32[]{:S(2)}) collective-permute-start(bf16[256,1024]{1,0:T(8,128)(2,1)} %get-tuple-element.33), channel_id=1, source_target_pairs={{4,8},{12,28},{20,24},{8,4},{16,0},{24,20},{5,9},{13,29},{21,25},{... | collective-permute-start | bytes 1572872 | tf_op jit(solution)/shard_map/ppermute | solution.py:423
  6.3 7.1 %collective-permute-start.4 = (bf16[192,1024]{1,0:T(8,128)(2,1)}, bf16[192,1024]{1,0:T(8,128)(2,1)}, u32[]{:S(2)}, u32[]{:S(2)}) collective-permute-start(bf16[192,1024]{1,0:T(8,128)(2,1)} %get-tuple-element.40), channel_id=1, source_target_pairs={{0,12},{8,20},{16,28},{12,0},{20,8},{28,16},{1,13},{9,21},{17,29},... | collective-permute-start | bytes 1179656 | tf_op jit(solution)/shard_map/ppermute | solution.py:424
  13.5 0.1 collective-permute-start.5
  13.5 3.9 %collective-permute-start.6 = (bf16[64,1024]{1,0:T(8,128)(2,1)}, bf16[64,1024]{1,0:T(8,128)(2,1)}, u32[]{:S(2)}, u32[]{:S(2)}) collective-permute-start(bf16[64,1024]{1,0:T(8,128)(2,1)} %get-tuple-element.42), channel_id=1, source_target_pairs={{24,0},{28,4},{0,24},{4,28},{25,1},{29,5},{1,25},{5,29},{26,2},{30... | collective-permute-start | bytes 393224 | tf_op jit(solution)/shard_map/ppermute | solution.py:431
  17.5 0.0 collective-permute-done.1.mk.mv
  17.5 1.5 %collective-permute-start.3 = (bf16[320,1024]{1,0:T(8,128)(2,1)}, bf16[320,1024]{1,0:T(8,128)(2,1)}, u32[]{:S(2)}, u32[]{:S(2)}) collective-permute-start(bf16[320,1024]{1,0:T(8,128)(2,1)} %get-tuple-element.39), channel_id=1, source_target_pairs={{4,8},{12,16},{20,24},{8,4},{16,12},{24,20},{5,9},{13,17},{21,25},... | collective-permute-start | bytes 1966088 | tf_op jit(solution)/shard_map/ppermute | solution.py:434
  19.0 10.2 %near.1 = (f32[1024,512]{1,0:T(8,128)}, f32[1024,128]{1,0:T(8,128)}) custom-call(s32[1]{0:T(128)} %bitcast.dev_ref, bf16[1024,512]{1,0:T(8,128)(2,1)} %q_ref.3, bf16[1024,512]{1,0:T(8,128)(2,1)} %k_ref.3, bf16[1024,512]{1,0:T(8,128)(2,1)} %v_ref.3, bf16[512,1024]{1,0:T(8,128)(2,1)} %get-tuple-element.34.l1k.l1v, ...), custom_call_target="tpu_custom_call" | custom-call | flops 2415919104 | bytes 12582912 | tf_op jit(solution)/shard_map/near/pallas_call | solution.py:453
  29.2 0.0 collective-permute-done.edge_ref
  29.2 2.7 %collective-permute-start.2 = (bf16[256,1024]{1,0:T(8,128)(2,1)}, bf16[256,1024]{1,0:T(8,128)(2,1)}, u32[]{:S(2)}, u32[]{:S(2)}) collective-permute-start(bf16[256,1024]{1,0:T(8,128)(2,1)} %collective-permute-done.edge_ref), channel_id=1, source_target_pairs={{28,16},{0,12},{29,17},{1,13},{30,18},{2,14},{31,19},{3,15}} | collective-permute-start | bytes 1572872 | tf_op jit(solution)/shard_map/ppermute | solution.py:477
  32.0 0.0 collective-permute-done.4.refs_4_.refs_5_
  32.0 0.0 collective-permute-done.5.refs_8_.refs_9_
  32.0 0.1 collective-permute-start.7
  32.1 0.5 collective-permute-start.8
  32.6 0.1 collective-permute-start.9
  32.6 2.2 %collective-permute-done.9.refs_14_.refs_15_ = bf16[64,1024]{1,0:T(8,128)(2,1)} collective-permute-done((bf16[64,1024]{1,0:T(8,128)(2,1)}, bf16[64,1024]{1,0:T(8,128)(2,1)}, u32[]{:S(2)}, u32[]{:S(2)}) %collective-permute-start.9) | collective-permute-done | bytes 131104 | tf_op jit(solution)/shard_map/ppermute | solution.py:481
  34.9 0.0 collective-permute-done.7.refs_6_.refs_7_
  34.9 0.0 collective-permute-done.8.refs_10_.refs_11_
  34.9 3.3 %collective-permute-done.2.via_ref = bf16[256,1024]{1,0:T(8,128)(2,1)} collective-permute-done((bf16[256,1024]{1,0:T(8,128)(2,1)}, bf16[256,1024]{1,0:T(8,128)(2,1)}, u32[]{:S(2)}, u32[]{:S(2)}) %collective-permute-start.2) | collective-permute-done | bytes 524320 | tf_op jit(solution)/shard_map/ppermute | solution.py:477
  38.2 2.8 %rim.1 = (bf16[896,1024]{1,0:T(8,128)(2,1)}, bf16[256,1024]{1,0:T(8,128)(2,1)}) custom-call(s32[1]{0:T(128)} %bitcast.dev_ref, bf16[256,1024]{1,0:T(8,128)(2,1)} %collective-permute-done.edge_ref, bf16[256,1024]{1,0:T(8,128)(2,1)} %collective-permute-done.2.via_ref, bf16[320,1024]{1,0:T(8,128)(2,1)} %collective-permute-done.3.x1_ref), custom_call_target="tpu_custom_call" | custom-call | tf_op jit(solution)/shard_map/rim/pallas_call | solution.py:483
  41.0 1.1 %collective-permute-start.10 = (bf16[256,1024]{1,0:T(8,128)(2,1)}, bf16[256,1024]{1,0:T(8,128)(2,1)}, u32[]{:S(2)}, u32[]{:S(2)}) collective-permute-start(bf16[256,1024]{1,0:T(8,128)(2,1)} %get-tuple-element.52), channel_id=1, source_target_pairs={{0,4},{4,0},{8,12},{12,8},{16,20},{20,16},{24,28},{28,24},{1,5},{5... | collective-permute-start | bytes 1572872 | tf_op jit(solution)/shard_map/ppermute | solution.py:493
  42.1 1.9 %collective-permute-done.10.refs_2_.refs_3_ = bf16[256,1024]{1,0:T(8,128)(2,1)} collective-permute-done((bf16[256,1024]{1,0:T(8,128)(2,1)}, bf16[256,1024]{1,0:T(8,128)(2,1)}, u32[]{:S(2)}, u32[]{:S(2)}) %collective-permute-start.10) | collective-permute-done | bytes 524320 | tf_op jit(solution)/shard_map/ppermute | solution.py:493
  44.0 9.4 %far.1 = bf16[1024,512]{1,0:T(8,128)(2,1)} custom-call(s32[1]{0:T(128)} %bitcast.dev_ref, bf16[1024,512]{1,0:T(8,128)(2,1)} %q_ref.3, bf16[896,1024]{1,0:T(8,128)(2,1)} %get-tuple-element.51.refs_0_.refs_1_, bf16[896,1024]{1,0:T(8,128)(2,1)} %get-tuple-element.51.refs_0_.refs_1_, bf16[256,1024]{1,0:T(8,128)(2,1)} %collective-permute-done.10.refs_2_.refs_3_, ...), custom_call_target="tpu_custom_call" | custom-call | flops 2281701376 | bytes 12582912 | tf_op jit(solution)/shard_map/far/pallas_call | solution.py:453
  (2 shorter events, 0.0 us)
Async XLA Ops:
  4.5 12.9 %collective-permute-start.1 = (bf16[896,1024]{1,0:T(8,128)(2,1)}, bf16[896,1024]{1,0:T(8,128)(2,1)}, u32[]{:S(2)}, u32[]{:S(2)}) collective-permute-start(bf16[896,1024]{1,0:T(8,128)(2,1)} %get-tuple-element.35), channel_id=1, source_target_pairs={{0,4},{4,0},{8,12},{12,8},{16,20},{20,16},{24,28},{28,24},{1,5},{5... | collective-permute-start | bytes 5505032 | tf_op jit(solution)/shard_map/ppermute | solution.py:436
  5.0 24.2 %collective-permute-start = (bf16[256,1024]{1,0:T(8,128)(2,1)}, bf16[256,1024]{1,0:T(8,128)(2,1)}, u32[]{:S(2)}, u32[]{:S(2)}) collective-permute-start(bf16[256,1024]{1,0:T(8,128)(2,1)} %get-tuple-element.33), channel_id=1, source_target_pairs={{4,8},{12,28},{20,24},{8,4},{16,0},{24,20},{5,9},{13,29},{21,25},{... | collective-permute-start | bytes 1572872 | tf_op jit(solution)/shard_map/ppermute | solution.py:423
  6.3 25.7 %collective-permute-start.4 = (bf16[192,1024]{1,0:T(8,128)(2,1)}, bf16[192,1024]{1,0:T(8,128)(2,1)}, u32[]{:S(2)}, u32[]{:S(2)}) collective-permute-start(bf16[192,1024]{1,0:T(8,128)(2,1)} %get-tuple-element.40), channel_id=1, source_target_pairs={{0,12},{8,20},{16,28},{12,0},{20,8},{28,16},{1,13},{9,21},{17,29},... | collective-permute-start | bytes 1179656 | tf_op jit(solution)/shard_map/ppermute | solution.py:424
  13.5 18.5 %collective-permute-start.5 = (bf16[192,1024]{1,0:T(8,128)(2,1)}, bf16[192,1024]{1,0:T(8,128)(2,1)}, u32[]{:S(2)}, u32[]{:S(2)}) collective-permute-start(bf16[192,1024]{1,0:T(8,128)(2,1)} %get-tuple-element.41), channel_id=1, source_target_pairs={{16,0},{20,4},{24,8},{28,12},{0,16},{4,20},{8,24},{12,28},{17,1},{... | collective-permute-start | bytes 1179656 | tf_op jit(solution)/shard_map/ppermute | solution.py:431
  13.5 18.4 %collective-permute-start.6 = (bf16[64,1024]{1,0:T(8,128)(2,1)}, bf16[64,1024]{1,0:T(8,128)(2,1)}, u32[]{:S(2)}, u32[]{:S(2)}) collective-permute-start(bf16[64,1024]{1,0:T(8,128)(2,1)} %get-tuple-element.42), channel_id=1, source_target_pairs={{24,0},{28,4},{0,24},{4,28},{25,1},{29,5},{1,25},{5,29},{26,2},{30... | collective-permute-start | bytes 393224 | tf_op jit(solution)/shard_map/ppermute | solution.py:431
  17.5 15.2 %collective-permute-start.3 = (bf16[320,1024]{1,0:T(8,128)(2,1)}, bf16[320,1024]{1,0:T(8,128)(2,1)}, u32[]{:S(2)}, u32[]{:S(2)}) collective-permute-start(bf16[320,1024]{1,0:T(8,128)(2,1)} %get-tuple-element.39), channel_id=1, source_target_pairs={{4,8},{12,16},{20,24},{8,4},{16,12},{24,20},{5,9},{13,17},{21,25},... | collective-permute-start | bytes 1966088 | tf_op jit(solution)/shard_map/ppermute | solution.py:434
  29.2 8.9 %collective-permute-start.2 = (bf16[256,1024]{1,0:T(8,128)(2,1)}, bf16[256,1024]{1,0:T(8,128)(2,1)}, u32[]{:S(2)}, u32[]{:S(2)}) collective-permute-start(bf16[256,1024]{1,0:T(8,128)(2,1)} %collective-permute-done.edge_ref), channel_id=1, source_target_pairs={{28,16},{0,12},{29,17},{1,13},{30,18},{2,14},{31,19},{3,15}} | collective-permute-start | bytes 1572872 | tf_op jit(solution)/shard_map/ppermute | solution.py:477
  32.0 2.9 %collective-permute-start.7 = (bf16[192,1024]{1,0:T(8,128)(2,1)}, bf16[192,1024]{1,0:T(8,128)(2,1)}, u32[]{:S(2)}, u32[]{:S(2)}) collective-permute-start(bf16[192,1024]{1,0:T(8,128)(2,1)} %collective-permute-done.4.refs_4_.refs_5_), channel_id=1, source_target_pairs={{0,4},{4,0},{8,12},{12,8},{16,20},{20,16},{24,28},{28,24},{1,5},{5... | collective-permute-start | bytes 1179656 | tf_op jit(solution)/shard_map/ppermute | solution.py:479
  32.1 2.8 %collective-permute-start.8 = (bf16[192,1024]{1,0:T(8,128)(2,1)}, bf16[192,1024]{1,0:T(8,128)(2,1)}, u32[]{:S(2)}, u32[]{:S(2)}) collective-permute-start(bf16[192,1024]{1,0:T(8,128)(2,1)} %collective-permute-done.5.refs_8_.refs_9_), channel_id=1, source_target_pairs={{0,4},{4,0},{8,12},{12,8},{16,20},{20,16},{24,28},{28,24},{1,5},{5... | collective-permute-start | bytes 1179656 | tf_op jit(solution)/shard_map/ppermute | solution.py:481
  32.6 2.3 %collective-permute-start.9 = (bf16[64,1024]{1,0:T(8,128)(2,1)}, bf16[64,1024]{1,0:T(8,128)(2,1)}, u32[]{:S(2)}, u32[]{:S(2)}) collective-permute-start(bf16[64,1024]{1,0:T(8,128)(2,1)} %collective-permute-done.6.refs_12_.refs_13_), channel_id=1, source_target_pairs={{0,4},{4,0},{8,12},{12,8},{16,20},{20,16},{24,28},{28,24},{1,5},{5... | collective-permute-start | bytes 393224 | tf_op jit(solution)/shard_map/ppermute | solution.py:481
  41.0 3.0 %collective-permute-start.10 = (bf16[256,1024]{1,0:T(8,128)(2,1)}, bf16[256,1024]{1,0:T(8,128)(2,1)}, u32[]{:S(2)}, u32[]{:S(2)}) collective-permute-start(bf16[256,1024]{1,0:T(8,128)(2,1)} %get-tuple-element.52), channel_id=1, source_target_pairs={{0,4},{4,0},{8,12},{12,8},{16,20},{20,16},{24,28},{28,24},{1,5},{5... | collective-permute-start | bytes 1572872 | tf_op jit(solution)/shard_map/ppermute | solution.py:493

commit v6 on v5

--- a/solution.py
+++ b/solution.py
@@ -467,7 +467,7 @@
     stats = attention(
         near_kernel,
         "near",
-        1152,
+        2500,
         [(key_rows, value_rows), l1, i1r],
         (),
     )

time: 53.8 us -> 53.4 us (level)
  starting transfers between devices: 18.9 us -> 18.3 us
    ppermute x1, starting transfers between devices: 7.14 us -> 1.92 us  [on_device(): lax.ppermute(x2s, 'ctx', [(i, i + 3) for i in range(0, count - 3, 2)] + [...]
    ppermute x2, starting transfers between devices: 3.99 us -> 8 us  [on_device(): lax.ppermute(ys if abs(shifts[0]) == 4 else l4, 'ctx', flow_pairs(shifts,...]
    ppermute x1, starting transfers between devices: 2.73 us -> 4.07 us  [on_device(): lax.ppermute(edge_r, 'ctx', [(via, t) for (_, t), via in detours.items()])]
    ppermute x1, starting transfers between devices: 1.11 us -> 0.37 us  [on_device(): i2r = lax.ppermute(i2s, 'ctx', mates)]
where the time goes in v6:
time: 53.4 us; the launch traced here: 52.9 us
  Pallas kernels  27 us (51%)
  starting transfers between devices  18.3 us (34%)
  waiting for transfers between devices  7.42 us (14%)
    pallas_call x2, Pallas kernels, attention(): pl.pallas_call(kernel, name=name, grid=(HEADS,), out_shape=shape(token_ro...  19.6 us
    ppermute x2, starting transfers between devices, on_device(): lax.ppermute(ys if abs(shifts[0]) == 4 else l4, 'ctx', flow_pairs(shifts,...  8 us
    pallas_call x1, Pallas kernels, on_device(): pl.pallas_call(pool_kernel, name='pool', grid=(2,), out_shape=[shape(rows...  4.52 us
    ppermute x1, starting transfers between devices, on_device(): lax.ppermute(edge_r, 'ctx', [(via, t) for (_, t), via in detours.items()])  4.07 us
    ppermute x1, waiting for transfers between devices, on_device(): lax.ppermute(edge_r, 'ctx', [(via, t) for (_, t), via in detours.items()])  3.3 us
    pallas_call x1, Pallas kernels, on_device(): pl.pallas_call(functools.partial(rim_kernel, [t for _, t in detours]), na...  2.82 us
    ppermute x2, waiting for transfers between devices, on_device(): tables += [yr, lax.ppermute(yr, 'ctx', mates)]  2.22 us
    ppermute x1, starting transfers between devices, on_device(): lax.ppermute(x2s, 'ctx', [(i, i + 3) for i in range(0, count - 3, 2)] + [...  1.92 us
  transfers between devices with their start and end apart: 11, of which 3 were waited for; matrix products, arithmetic and copies ran while one was open for 0% of the time, Pallas kernels for 19%

profile of v6, /device:TPU:0, one launch (start us, length us, event | category | flops | bytes accessed | tf_op | source)
XLA Modules:
  0.0 52.9 jit_solution(12491278354831436227)
XLA Ops:
  0.0 4.5 %pool.1 = (bf16[256,1024]{1,0:T(8,128)(2,1)}, bf16[320,1024]{1,0:T(8,128)(2,1)}, bf16[896,1024]{1,0:T(8,128)(2,1)}, bf16[192,1024]{1,0:T(8,128)(2,1)}, bf16[192,...) custom-call(s32[1]{0:T(128)} %bitcast.dev_ref, bf16[1024,512]{1,0:T(8,128)(2,1)} %k_ref.3, ...), custom_call_target="tpu_custom_call" | custom-call | bytes 25165824 | tf_op jit(solution)/shard_map/pool/pallas_call | solution.py:407
  4.5 0.5 collective-permute-start.1
  5.0 1.3 %collective-permute-start = (bf16[256,1024]{1,0:T(8,128)(2,1)}, bf16[256,1024]{1,0:T(8,128)(2,1)}, u32[]{:S(2)}, u32[]{:S(2)}) collective-permute-start(bf16[256,1024]{1,0:T(8,128)(2,1)} %get-tuple-element.33), channel_id=1, source_target_pairs={{4,8},{12,28},{20,24},{8,4},{16,0},{24,20},{5,9},{13,29},{21,25},{... | collective-permute-start | bytes 1572872 | tf_op jit(solution)/shard_map/ppermute | solution.py:423
  6.3 6.6 %collective-permute-start.6 = (bf16[64,1024]{1,0:T(8,128)(2,1)}, bf16[64,1024]{1,0:T(8,128)(2,1)}, u32[]{:S(2)}, u32[]{:S(2)}) collective-permute-start(bf16[64,1024]{1,0:T(8,128)(2,1)} %get-tuple-element.42), channel_id=1, source_target_pairs={{24,0},{28,4},{0,24},{4,28},{25,1},{29,5},{1,25},{5,29},{26,2},{30... | collective-permute-start | bytes 393224 | tf_op jit(solution)/shard_map/ppermute | solution.py:431
  12.9 1.9 %collective-permute-start.4 = (bf16[192,1024]{1,0:T(8,128)(2,1)}, bf16[192,1024]{1,0:T(8,128)(2,1)}, u32[]{:S(2)}, u32[]{:S(2)}) collective-permute-start(bf16[192,1024]{1,0:T(8,128)(2,1)} %get-tuple-element.40), channel_id=1, source_target_pairs={{0,12},{8,20},{16,28},{12,0},{20,8},{28,16},{1,13},{9,21},{17,29},... | collective-permute-start | bytes 1179656 | tf_op jit(solution)/shard_map/ppermute | solution.py:424
  14.9 1.4 %collective-permute-start.5 = (bf16[192,1024]{1,0:T(8,128)(2,1)}, bf16[192,1024]{1,0:T(8,128)(2,1)}, u32[]{:S(2)}, u32[]{:S(2)}) collective-permute-start(bf16[192,1024]{1,0:T(8,128)(2,1)} %get-tuple-element.41), channel_id=1, source_target_pairs={{16,0},{20,4},{24,8},{28,12},{0,16},{4,20},{8,24},{12,28},{17,1},{... | collective-permute-start | bytes 1179656 | tf_op jit(solution)/shard_map/ppermute | solution.py:431
  16.2 0.0 collective-permute-done.1.mk.mv
  16.2 1.5 %collective-permute-start.3 = (bf16[320,1024]{1,0:T(8,128)(2,1)}, bf16[320,1024]{1,0:T(8,128)(2,1)}, u32[]{:S(2)}, u32[]{:S(2)}) collective-permute-start(bf16[320,1024]{1,0:T(8,128)(2,1)} %get-tuple-element.39), channel_id=1, source_target_pairs={{4,8},{12,16},{20,24},{8,4},{16,12},{24,20},{5,9},{13,17},{21,25},... | collective-permute-start | bytes 1966088 | tf_op jit(solution)/shard_map/ppermute | solution.py:434
  17.7 10.2 %near.1 = (f32[1024,512]{1,0:T(8,128)}, f32[1024,128]{1,0:T(8,128)}) custom-call(s32[1]{0:T(128)} %bitcast.dev_ref, bf16[1024,512]{1,0:T(8,128)(2,1)} %q_ref.3, bf16[1024,512]{1,0:T(8,128)(2,1)} %k_ref.3, bf16[1024,512]{1,0:T(8,128)(2,1)} %v_ref.3, bf16[512,1024]{1,0:T(8,128)(2,1)} %get-tuple-element.34.l1k.l1v, ...), custom_call_target="tpu_custom_call" | custom-call | flops 5242880000 | bytes 12582912 | tf_op jit(solution)/shard_map/near/pallas_call | solution.py:453
  28.0 0.0 collective-permute-done.edge_ref
  28.0 4.1 %collective-permute-start.2 = (bf16[256,1024]{1,0:T(8,128)(2,1)}, bf16[256,1024]{1,0:T(8,128)(2,1)}, u32[]{:S(2)}, u32[]{:S(2)}) collective-permute-start(bf16[256,1024]{1,0:T(8,128)(2,1)} %collective-permute-done.edge_ref), channel_id=1, source_target_pairs={{28,16},{0,12},{29,17},{1,13},{30,18},{2,14},{31,19},{3,15}} | collective-permute-start | bytes 1572872 | tf_op jit(solution)/shard_map/ppermute | solution.py:477
  32.0 0.0 collective-permute-done.6.refs_12_.refs_13_
  32.1 0.0 collective-permute-done.4.refs_4_.refs_5_
  32.1 0.0 collective-permute-done.5.refs_8_.refs_9_
  32.1 0.1 collective-permute-start.7
  32.1 0.5 collective-permute-start.8
  32.6 0.1 collective-permute-start.9
  32.7 0.0 collective-permute-done.3.x1_ref
  32.7 2.2 %collective-permute-done.9.refs_14_.refs_15_ = bf16[64,1024]{1,0:T(8,128)(2,1)} collective-permute-done((bf16[64,1024]{1,0:T(8,128)(2,1)}, bf16[64,1024]{1,0:T(8,128)(2,1)}, u32[]{:S(2)}, u32[]{:S(2)}) %collective-permute-start.9) | collective-permute-done | bytes 131104 | tf_op jit(solution)/shard_map/ppermute | solution.py:481
  34.9 3.3 %collective-permute-done.2.via_ref = bf16[256,1024]{1,0:T(8,128)(2,1)} collective-permute-done((bf16[256,1024]{1,0:T(8,128)(2,1)}, bf16[256,1024]{1,0:T(8,128)(2,1)}, u32[]{:S(2)}, u32[]{:S(2)}) %collective-permute-start.2) | collective-permute-done | bytes 524320 | tf_op jit(solution)/shard_map/ppermute | solution.py:477
  38.2 2.8 %rim.1 = (bf16[896,1024]{1,0:T(8,128)(2,1)}, bf16[256,1024]{1,0:T(8,128)(2,1)}) custom-call(s32[1]{0:T(128)} %bitcast.dev_ref, bf16[256,1024]{1,0:T(8,128)(2,1)} %collective-permute-done.edge_ref, bf16[256,1024]{1,0:T(8,128)(2,1)} %collective-permute-done.2.via_ref, bf16[320,1024]{1,0:T(8,128)(2,1)} %collective-permute-done.3.x1_ref), custom_call_target="tpu_custom_call" | custom-call | tf_op jit(solution)/shard_map/rim/pallas_call | solution.py:483
  41.1 0.4 collective-permute-start.10
  41.4 1.9 %collective-permute-done.10.refs_2_.refs_3_ = bf16[256,1024]{1,0:T(8,128)(2,1)} collective-permute-done((bf16[256,1024]{1,0:T(8,128)(2,1)}, bf16[256,1024]{1,0:T(8,128)(2,1)}, u32[]{:S(2)}, u32[]{:S(2)}) %collective-permute-start.10) | collective-permute-done | bytes 524320 | tf_op jit(solution)/shard_map/ppermute | solution.py:493
  43.3 9.4 %far.1 = bf16[1024,512]{1,0:T(8,128)(2,1)} custom-call(s32[1]{0:T(128)} %bitcast.dev_ref, bf16[1024,512]{1,0:T(8,128)(2,1)} %q_ref.3, bf16[896,1024]{1,0:T(8,128)(2,1)} %get-tuple-element.51.refs_0_.refs_1_, bf16[896,1024]{1,0:T(8,128)(2,1)} %get-tuple-element.51.refs_0_.refs_1_, bf16[256,1024]{1,0:T(8,128)(2,1)} %collective-permute-done.10.refs_2_.refs_3_, ...), custom_call_target="tpu_custom_call" | custom-call | flops 2281701376 | bytes 12582912 | tf_op jit(solution)/shard_map/far/pallas_call | solution.py:453
  (2 shorter events, 0.0 us)
Async XLA Ops:
  4.5 11.7 %collective-permute-start.1 = (bf16[896,1024]{1,0:T(8,128)(2,1)}, bf16[896,1024]{1,0:T(8,128)(2,1)}, u32[]{:S(2)}, u32[]{:S(2)}) collective-permute-start(bf16[896,1024]{1,0:T(8,128)(2,1)} %get-tuple-element.35), channel_id=1, source_target_pairs={{0,4},{4,0},{8,12},{12,8},{16,20},{20,16},{24,28},{28,24},{1,5},{5... | collective-permute-start | bytes 5505032 | tf_op jit(solution)/shard_map/ppermute | solution.py:436
  5.0 23.0 %collective-permute-start = (bf16[256,1024]{1,0:T(8,128)(2,1)}, bf16[256,1024]{1,0:T(8,128)(2,1)}, u32[]{:S(2)}, u32[]{:S(2)}) collective-permute-start(bf16[256,1024]{1,0:T(8,128)(2,1)} %get-tuple-element.33), channel_id=1, source_target_pairs={{4,8},{12,28},{20,24},{8,4},{16,0},{24,20},{5,9},{13,29},{21,25},{... | collective-permute-start | bytes 1572872 | tf_op jit(solution)/shard_map/ppermute | solution.py:423
  6.3 25.7 %collective-permute-start.6 = (bf16[64,1024]{1,0:T(8,128)(2,1)}, bf16[64,1024]{1,0:T(8,128)(2,1)}, u32[]{:S(2)}, u32[]{:S(2)}) collective-permute-start(bf16[64,1024]{1,0:T(8,128)(2,1)} %get-tuple-element.42), channel_id=1, source_target_pairs={{24,0},{28,4},{0,24},{4,28},{25,1},{29,5},{1,25},{5,29},{26,2},{30... | collective-permute-start | bytes 393224 | tf_op jit(solution)/shard_map/ppermute | solution.py:431
  12.9 19.1 %collective-permute-start.4 = (bf16[192,1024]{1,0:T(8,128)(2,1)}, bf16[192,1024]{1,0:T(8,128)(2,1)}, u32[]{:S(2)}, u32[]{:S(2)}) collective-permute-start(bf16[192,1024]{1,0:T(8,128)(2,1)} %get-tuple-element.40), channel_id=1, source_target_pairs={{0,12},{8,20},{16,28},{12,0},{20,8},{28,16},{1,13},{9,21},{17,29},... | collective-permute-start | bytes 1179656 | tf_op jit(solution)/shard_map/ppermute | solution.py:424
  14.9 17.2 %collective-permute-start.5 = (bf16[192,1024]{1,0:T(8,128)(2,1)}, bf16[192,1024]{1,0:T(8,128)(2,1)}, u32[]{:S(2)}, u32[]{:S(2)}) collective-permute-start(bf16[192,1024]{1,0:T(8,128)(2,1)} %get-tuple-element.41), channel_id=1, source_target_pairs={{16,0},{20,4},{24,8},{28,12},{0,16},{4,20},{8,24},{12,28},{17,1},{... | collective-permute-start | bytes 1179656 | tf_op jit(solution)/shard_map/ppermute | solution.py:431
  16.2 16.5 %collective-permute-start.3 = (bf16[320,1024]{1,0:T(8,128)(2,1)}, bf16[320,1024]{1,0:T(8,128)(2,1)}, u32[]{:S(2)}, u32[]{:S(2)}) collective-permute-start(bf16[320,1024]{1,0:T(8,128)(2,1)} %get-tuple-element.39), channel_id=1, source_target_pairs={{4,8},{12,16},{20,24},{8,4},{16,12},{24,20},{5,9},{13,17},{21,25},... | collective-permute-start | bytes 1966088 | tf_op jit(solution)/shard_map/ppermute | solution.py:434
  28.0 10.3 %collective-permute-start.2 = (bf16[256,1024]{1,0:T(8,128)(2,1)}, bf16[256,1024]{1,0:T(8,128)(2,1)}, u32[]{:S(2)}, u32[]{:S(2)}) collective-permute-start(bf16[256,1024]{1,0:T(8,128)(2,1)} %collective-permute-done.edge_ref), channel_id=1, source_target_pairs={{28,16},{0,12},{29,17},{1,13},{30,18},{2,14},{31,19},{3,15}} | collective-permute-start | bytes 1572872 | tf_op jit(solution)/shard_map/ppermute | solution.py:477
  32.1 2.9 %collective-permute-start.7 = (bf16[192,1024]{1,0:T(8,128)(2,1)}, bf16[192,1024]{1,0:T(8,128)(2,1)}, u32[]{:S(2)}, u32[]{:S(2)}) collective-permute-start(bf16[192,1024]{1,0:T(8,128)(2,1)} %collective-permute-done.4.refs_4_.refs_5_), channel_id=1, source_target_pairs={{0,4},{4,0},{8,12},{12,8},{16,20},{20,16},{24,28},{28,24},{1,5},{5... | collective-permute-start | bytes 1179656 | tf_op jit(solution)/shard_map/ppermute | solution.py:479
  32.1 2.8 %collective-permute-start.8 = (bf16[192,1024]{1,0:T(8,128)(2,1)}, bf16[192,1024]{1,0:T(8,128)(2,1)}, u32[]{:S(2)}, u32[]{:S(2)}) collective-permute-start(bf16[192,1024]{1,0:T(8,128)(2,1)} %collective-permute-done.5.refs_8_.refs_9_), channel_id=1, source_target_pairs={{0,4},{4,0},{8,12},{12,8},{16,20},{20,16},{24,28},{28,24},{1,5},{5... | collective-permute-start | bytes 1179656 | tf_op jit(solution)/shard_map/ppermute | solution.py:481
  32.6 2.3 %collective-permute-start.9 = (bf16[64,1024]{1,0:T(8,128)(2,1)}, bf16[64,1024]{1,0:T(8,128)(2,1)}, u32[]{:S(2)}, u32[]{:S(2)}) collective-permute-start(bf16[64,1024]{1,0:T(8,128)(2,1)} %collective-permute-done.6.refs_12_.refs_13_), channel_id=1, source_target_pairs={{0,4},{4,0},{8,12},{12,8},{16,20},{20,16},{24,28},{28,24},{1,5},{5... | collective-permute-start | bytes 393224 | tf_op jit(solution)/shard_map/ppermute | solution.py:481
  41.1 2.3 %collective-permute-start.10 = (bf16[256,1024]{1,0:T(8,128)(2,1)}, bf16[256,1024]{1,0:T(8,128)(2,1)}, u32[]{:S(2)}, u32[]{:S(2)}) collective-permute-start(bf16[256,1024]{1,0:T(8,128)(2,1)} %get-tuple-element.52), channel_id=1, source_target_pairs={{0,4},{4,0},{8,12},{12,8},{16,20},{20,16},{24,28},{28,24},{1,5},{5... | collective-permute-start | bytes 1572872 | tf_op jit(solution)/shard_map/ppermute | solution.py:493
